TPU v7x, 32 devices: a whole 2x2x4 slice. The times are simulated.
32 devices in a mesh: parts: 2 (over x), rows: 16 (over z, y, core).
Axes of the slice: x: 2, y: 2, z: 4, core: 2. Of those that a mesh axis runs over, the one named last changes fastest.
Arguments:
- estimate: float32 [256, 2048], P(('parts', 'rows')), parts along dimension 0, may hold values from -6 to 6
- observed: float32 [256, 2048], P('parts', 'rows'), parts along dimension 0, may hold values from -6 to 6
- cotangent: float32 [256, 2048], P(('parts', 'rows')), parts along dimension 0
- zone_map: int32 [2, 16], P('parts'), parts along dimension 0, may hold values from 0 to 7
- bank_pick: int32 [2, 8], replicated, may hold values from 0 to 7
- psf_bank: float32 [8, 25], replicated, may hold values from 0.01 to 1
- w_first: bfloat16 [32, 1, 3, 3], replicated, may hold values from -2 to 2
- w_mid: bfloat16 [32, 32, 3, 3], replicated, may hold values from -0.375 to 0.375
- w_last: bfloat16 [1, 32, 3, 3], replicated, may hold values from -0.375 to 0.375
Outputs:
- denoised: float32 [256, 2048], P(('parts', 'rows')), parts along dimension 0
- grad_estimate: float32 [256, 2048], P(('parts', 'rows')), parts along dimension 0
- grad_first: float32 [64, 1, 3, 3], P('parts'), parts along dimension 0
- grad_mid: float32 [64, 32, 3, 3], P('parts'), parts along dimension 0
- grad_last: float32 [2, 32, 3, 3], P('parts'), parts along dimension 0
There are 2 independent parts, one for each index of `parts`. A program takes and returns all parts, laid end to end along the dimension named above; an argument that names none is the same for every part. Nothing has to cross between parts.
All inputs are finite; a program needn't handle non-finite values.
Results may differ from a plain program's by a relative error of at most 0.0071.
Values may be sent and summed in bfloat16 or wider, within the bound.
A program may use at most 256 MiB of HBM per device.

v0:
```python
import math

import jax
import jax.numpy as jnp
from jax import lax
from jax.sharding import PartitionSpec as P

BLK = 128
RAD = 12


STEP_SIZE = 2.0
GRAD_FACTOR = 8.0


def padded_2(shard, sides, width):
    for axis, dim in sides:
        size, length = (lax.axis_size(axis), shard.shape[dim])
        up = [(i, (i + 1) % size) for i in range(size - 1)]
        down = [(j, i) for i, j in up]
        last = lax.slice_in_dim(shard, length - width, length, axis=dim)
        leading = lax.slice_in_dim(shard, 0, width, axis=dim)
        before = lax.ppermute(last, axis, up)
        after = lax.ppermute(leading, axis, down)
        shard = jnp.concatenate([before, shard, after], axis=dim)
    return shard


def silu_slope(values):
    sigmoid = jax.nn.sigmoid(values)
    return sigmoid * (1.0 + values * (1.0 - sigmoid))


def flipped(weight):
    return jnp.transpose(jnp.flip(weight, (2, 3)), (1, 0, 2, 3))


def conv_rim(padded, weight):
    padding = ((0, 0), (1, 1))
    result = lax.conv_general_dilated(
        padded[None],
        weight,
        (1, 1),
        padding,
        dimension_numbers=("NCHW", "OIHW", "NCHW"),
        preferred_element_type=jnp.float32,
    )
    return result[0]


def weight_taps(framed, errors):
    height_cells = errors.shape[1]
    width_cells = errors.shape[2]
    all_taps = []
    for tap_row in range(3):
        line_taps = []
        for tap_col in range(3):
            window = framed[:, tap_row : tap_row + height_cells, tap_col : tap_col + width_cells]
            line_taps.append(
                jnp.einsum("ohw,chw->oc", errors, window, preferred_element_type=jnp.float32)
            )
        all_taps.append(jnp.stack(line_taps, axis=-1))
    return jnp.stack(all_taps, axis=-2)


def weight_grad(padded, errors, rim_dim):
    widths = [(0, 0), (0, 0), (0, 0)]
    widths[3 - rim_dim] = (1, 1)
    framed = jnp.pad(padded, widths)
    return weight_taps(framed, errors)


def blur_line(values, tap_coef, along, adjoint):
    length = values.shape[along]
    widths = [(0, 0), (0, 0)]
    widths[along] = (RAD, RAD)
    summed = jnp.zeros_like(values)
    padded = jnp.pad(values, widths)
    for offset in range(2 * RAD + 1):
        factor = tap_coef[offset][None, :] if along == 1 else tap_coef[offset][:, None]
        if adjoint:
            spread = jnp.pad(factor * values, widths)
            summed = summed + lax.slice_in_dim(
                spread, 2 * RAD - offset, 2 * RAD - offset + length, axis=along
            )
        else:
            summed = summed + factor * lax.slice_in_dim(padded, offset, offset + length, axis=along)
    return summed


def zone_kernels(psf_bank, bank_pick):
    norm_bank = psf_bank / jnp.sum(psf_bank, axis=1, keepdims=True)
    select = (
        bank_pick[:, :, None] == jnp.arange(psf_bank.shape[0], dtype=jnp.int32)[None, None, :]
    ).astype(jnp.float32)
    return jnp.einsum("rzb,bt->rzt", select, norm_bank, precision=lax.Precision.HIGHEST)


def tap_table(zone_line, kernel_table):
    zone_count = kernel_table.shape[0]
    onehot = (zone_line[:, None] == jnp.arange(zone_count, dtype=jnp.int32)[None, :]).astype(
        jnp.float32
    )
    per_block = jnp.einsum("nz,zt->tn", onehot, kernel_table, precision=lax.Precision.HIGHEST)
    tap_count = per_block.shape[0]
    block_count = per_block.shape[1]
    return jnp.broadcast_to(per_block[:, :, None], (tap_count, block_count, BLK)).reshape(
        tap_count, block_count * BLK
    )


def data_gradient(values, target, row_coef, col_coef):
    blurred = blur_line(values, row_coef, 1, False)
    columns = lax.all_to_all(blurred, "rows", split_axis=1, concat_axis=0, tiled=True)
    columns = blur_line(columns, col_coef, 0, False)
    if target is not None:
        columns = columns - target
    spread = blur_line(columns, col_coef, 0, True)
    back_rows = lax.all_to_all(spread, "rows", split_axis=0, concat_axis=1, tiled=True)
    return blur_line(back_rows, row_coef, 1, True)


def band_rims(values):
    return padded_2(values, (("rows", 1),), 1)


def denoise(data_step, cotangent, w_first, w_mid, w_last, add_rims, rim_dim):
    first_in = data_step.astype(jnp.bfloat16)[None]
    first_pad = add_rims(first_in)
    pre_first = conv_rim(first_pad, w_first)
    act_first = jax.nn.silu(pre_first).astype(jnp.bfloat16)
    first_act_pad = add_rims(act_first)
    pre_mid = conv_rim(first_act_pad, w_mid)
    act_mid = jax.nn.silu(pre_mid).astype(jnp.bfloat16)
    mid_act_pad = add_rims(act_mid)
    denoised = data_step + conv_rim(mid_act_pad, w_last)[0]
    cot_in = cotangent.astype(jnp.bfloat16)[None]
    cot_pad = add_rims(cot_in)
    back_mid = (conv_rim(cot_pad, flipped(w_last)) * silu_slope(pre_mid)).astype(jnp.bfloat16)
    back_mid_pad = add_rims(back_mid)
    back_first = (conv_rim(back_mid_pad, flipped(w_mid)) * silu_slope(pre_first)).astype(
        jnp.bfloat16
    )
    back_first_pad = add_rims(back_first)
    grad_data = cotangent + conv_rim(back_first_pad, flipped(w_first))[0]
    grad_last = weight_grad(mid_act_pad, cot_in, rim_dim)
    grad_mid = weight_grad(first_act_pad, back_mid, rim_dim)
    grad_first = weight_grad(first_pad, back_first, rim_dim)
    return (denoised, grad_data, (grad_first, grad_mid, grad_last))


def on_device(estimate, observed, cotangent, zone_map, bank_pick, psf_bank, w_first, w_mid, w_last):
    band_rows = estimate.shape[0]
    width = estimate.shape[1]
    group_cols = observed.shape[1]
    position = lax.axis_index("rows")
    height = band_rows * lax.axis_size("rows")
    kernels = zone_kernels(psf_bank, bank_pick)
    col_line = lax.dynamic_slice_in_dim(zone_map, position * group_cols // BLK, 1, 1)[:, 0]
    col_coef = tap_table(col_line, kernels[1])
    row_line = lax.dynamic_slice_in_dim(zone_map, position * band_rows // BLK, 1, 0)[0]
    row_coef = tap_table(row_line, kernels[0])
    data_step = estimate - STEP_SIZE * data_gradient(estimate, observed, row_coef, col_coef)
    denoised, grad_data, partial_grads = denoise(
        data_step, cotangent, w_first, w_mid, w_last, band_rims, 1
    )
    grad_estimate = grad_data - STEP_SIZE * data_gradient(grad_data, None, row_coef, col_coef)
    grad_scale = GRAD_FACTOR / math.sqrt(height * width)
    grad_first, grad_mid, grad_last = lax.psum(
        (
            partial_grads[0] * grad_scale,
            partial_grads[1] * grad_scale,
            partial_grads[2] * grad_scale,
        ),
        "rows",
    )
    return (denoised, grad_estimate, grad_first, grad_mid, grad_last)


def solution(mesh):
    placed = (
        P(("parts", "rows"), None),
        P("parts", "rows"),
        P(("parts", "rows"), None),
        P("parts", None),
        P(),
        P(),
        P(),
        P(),
        P(),
    )
    return jax.shard_map(
        on_device,
        mesh=mesh,
        in_specs=placed,
        out_specs=(
            P(("parts", "rows"), None),
            P(("parts", "rows"), None),
            P("parts", None, None, None),
            P("parts", None, None, None),
            P("parts", None, None, None),
        ),
        check_vma=False,
    )
```

profile of v0, /device:TPU:0, one launch (start us, length us, event | category | flops | bytes accessed | tf_op | source)
XLA Modules:
  0.0 456.1 jit_solution(8213222737690068692)
XLA Ops:
  1.5 2.4 collective-permute-start.6
  9.5 3.6 add_bitcast_fusion.1
  13.1 9.3 %all-to-all-start = ((f32[8,16,128]{2,0,1:T(8,128)}), f32[8,16,128]{2,0,1:T(8,128)S(1)}, u32[]{:S(2)}, u32[]{:S(2)}) async-start(f32[8,16,128]{2,0,1:T(8,128)} %add_bitcast_fusion.1), calls=%async_computation | async-start | bytes 131072 | tf_op jit(solution)/shard_map/all_to_all | solution.py:114
  27.3 2.0 all-to-all-done
  29.3 16.7 %broadcast_multiply_fusion.47 = (f32[128,128]{1,0:T(8,128)S(1)}, f32[128,128]{1,0:T(8,128)S(1)}) fusion(f32[]{:T(128)} %bitcast.9, f32[128,128]{1,0:T(8,128)} %param.10, f32[]{:T(128)} %bitcast.61, f32[]{:T(128)} %bitcast.60, f32[]{:T(128)} %bitcast.59, f32[]{:T(128)} %bitcast.58, f32[]{:T(128)} %bitcast.57, f32[]{:T(128)} %bitcast.56, f32[]{:T(128)} %bitcast.55, ...), kind=kLoop, calls=%fused_computation.672 | loop fusion | flops 835584 | bytes 262244 | tf_op jit(solution)/shard_map/mul | solution.py:82
  46.1 3.3 broadcast_multiply_fusion.43
  49.4 11.4 %broadcast_multiply_fusion.45 = (f32[128,128]{1,0:T(8,128)S(1)}, f32[128,128]{1,0:T(8,128)S(1)}, f32[128,128]{1,0:T(8,128)S(1)}, f32[128,128]{1,0:T(8,128)S(1)},...) fusion(f32[128,128]{1,0:T(8,128)S(1)} %get-tuple-element.38, ...), kind=kLoop, calls=%fused_computation.670 | loop fusion | flops 294912 | bytes 1245256 | tf_op jit(solution)/shard_map/mul | solution.py:82
  60.8 1.4 fusion.342
  62.2 4.1 all-to-all-start.1
  67.9 5.3 %all-to-all-done.1 = f32[16,8,128]{2,1,0:T(8,128)S(1)} async-done(((f32[16,8,128]{2,1,0:T(8,128)}), f32[16,8,128]{2,1,0:T(8,128)S(1)}, u32[]{:S(2)}, u32[]{:S(2)}) %all-to-all-start.1) | async-done | bytes 65568 | tf_op jit(solution)/shard_map/all_to_all | solution.py:119
  74.8 1.5 collective-permute-start
  76.2 1.5 collective-permute-start.1
  77.7 7.6 %fusion.358 = f32[8,8,257,32]{3,1,2,0:T(8,128)} fusion(bf16[1,10,8,259]{2,0,3,1:T(2,128)(2,1)S(1)} %copy.104, bf16[32,1,3,3]{0,3,2,1:T(4,128)(2,1)S(1)} %bitcast.471), kind=kOutput, calls=%fused_computation.709 | convolution fusion | flops 9474048 | bytes 2147360 | tf_op jit(solution)/shard_map/conv_general_dilated | solution.py:40
  85.3 7.2 %copy.106 = f32[8,8,257,32]{2,3,1,0:T(8,128)} copy(f32[8,8,257,32]{3,1,2,0:T(8,128)} %fusion.358) | data formatting | bytes 4210688 | tf_op jit(solution)/shard_map/conv_general_dilated | solution.py:40
  94.8 7.6 %fusion.361 = f32[8,8,257,32]{3,1,2,0:T(8,128)} fusion(bf16[1,10,8,259]{2,0,3,1:T(2,128)(2,1)S(1)} %copy.92, bf16[32,1,3,3]{0,3,2,1:T(4,128)(2,1)S(1)} %copy-done.80), kind=kOutput, calls=%fused_computation.712 | convolution fusion | flops 9474048 | bytes 2147360 | tf_op jit(solution)/shard_map/conv_general_dilated | solution.py:40
  102.5 5.9 %copy.94 = f32[8,8,257,32]{2,3,1,0:T(8,128)S(1)} copy(f32[8,8,257,32]{3,1,2,0:T(8,128)} %fusion.361) | data formatting | bytes 4210688 | tf_op jit(solution)/shard_map/conv_general_dilated | solution.py:40
  110.0 3.4 copy.95
  113.4 3.0 reshape.463
  117.0 3.2 collective-permute-start.2
  122.2 2.5 collective-permute-done.3
  125.0 1.7 pad.422
  126.6 4.9 %reshape.468 = bf16[32,10,1,8,257]{4,3,0,1,2:T(8,128)(2,1)} reshape(bf16[32,10,1,2056]{3,0,1,2:T(8,128)(2,1)} %pad.422) | data formatting | bytes 2631680 | tf_op jit(solution)/shard_map/conv_general_dilated | solution.py:40
  131.6 7.5 %copy.97 = bf16[32,10,1,8,257]{0,3,4,1,2:T(8,128)(2,1)} copy(bf16[32,10,1,8,257]{4,3,0,1,2:T(8,128)(2,1)} %reshape.468) | data formatting | bytes 2631680 | tf_op jit(solution)/shard_map/conv_general_dilated | solution.py:40
  139.9 11.1 %fusion.6 = f32[8,8,257,32]{3,1,2,0:T(8,128)} fusion(bf16[32,32,3,3]{1,0,3,2:T(8,128)(2,1)S(1)} %copy-done, bf16[32,10,1,7,2]{0,3,4,1,2:T(8,128)(2,1)S(1)} %slice.1495, bf16[32,10,1,8,257]{0,3,4,1,2:T(8,128)(2,1)} %copy.97), kind=kOutput, calls=%fused_computation.7 | convolution fusion | flops 307147776 | bytes 3448576 | tf_op jit(solution)/shard_map/conv_general_dilated | solution.py:40
  151.0 7.1 %copy.98 = f32[8,8,257,32]{2,3,1,0:T(8,128)} copy(f32[8,8,257,32]{3,1,2,0:T(8,128)} %fusion.6) | data formatting | bytes 4210688 | tf_op jit(solution)/shard_map/conv_general_dilated | solution.py:40
  158.1 6.4 %multiply_convert_fusion.1 = (bf16[8,8,257,32]{2,3,1,0:T(8,128)(2,1)}, f32[8,8,257,32]{2,3,1,0:T(8,128)S(1)}, f32[8,8,257,32]{2,3,1,0:T(8,128)}) fusion(f32[8,8,257,32]{2,3,1,0:T(8,128)} %copy.98, pred[8,257]{1,0:T(8,128)(4,1)S(1)} %copy-done.79, f32[8,8,257,32]{2,3,1,0:T(8,128)} %copy.106), kind=kLoop, calls=%fused_computation.32 | loop fusion | flops 5789696 | bytes 9476104 | tf_op jit(solution)/shard_map/convert_element_type | solution.py:139
  164.5 3.4 copy.107
  167.9 4.2 reshape.486
  172.0 5.3 %copy.99 = f32[8,8,257,32]{2,1,3,0:T(8,128)} copy(f32[8,8,257,32]{2,3,1,0:T(8,128)} %get-tuple-element.41) | data formatting | bytes 4210688 | tf_op jit(solution)/shard_map/conv_general_dilated | solution.py:40
  177.3 4.6 reshape.472
  181.9 4.2 fusion.43
  192.2 2.0 reshape.488
  194.2 1.8 fusion.416
  196.0 6.1 %collective-permute-start.4 = (bf16[32,1,2048]{2,0,1:T(8,128)(2,1)}, bf16[32,1,2048]{2,0,1:T(8,128)(2,1)}, u32[]{:S(2)}, u32[]{:S(2)}) collective-permute-start(bf16[32,1,2048]{2,0,1:T(8,128)(2,1)} %get-tuple-element.55), channel_id=1, source_target_pairs={{0,1},{1,2},{2,3},{3,4},{4,5},{5,6},{6,7},{7,8},{8,9},{9,10},{10,1... | collective-permute-start | bytes 393224 | tf_op jit(solution)/shard_map/ppermute | solution.py:23
  203.4 3.0 collective-permute-start.8
  207.7 1.6 fusion.58
  212.2 2.5 reshape.491
  214.7 2.6 pad_maximum_fusion.1
  217.8 3.3 reshape.475
  221.1 7.5 %copy.101 = bf16[32,10,1,8,257]{0,3,4,1,2:T(8,128)(2,1)} copy(bf16[32,10,1,8,257]{4,3,0,1,2:T(8,128)(2,1)} %reshape.475) | data formatting | bytes 2631680 | tf_op jit(solution)/shard_map/conv_general_dilated | solution.py:40
  229.5 11.8 %broadcast_select_fusion.1 = f32[8,8,257,1]{3,1,2,0:T(8,128)} fusion(pred[8,257]{0,1:T(8,128)(4,1)S(1)} %copy-done.82, bf16[32,10,1,7,2]{0,3,4,1,2:T(8,128)(2,1)S(1)} %slice.1499, bf16[32,10,1,8,257]{0,3,4,1,2:T(8,128)(2,1)} %copy.101, bf16[1,32,3,3]{1,3,2,0:T(4,128)(2,1)S(1)} %copy-done.81), kind=kOutput, calls=%fused_computation.30 | convolution fusion | flops 13468736 | bytes 1393224 | tf_op jit(solution)/shard_map/conv_general_dilated | solution.py:40
  241.2 6.1 %copy.103 = f32[8,8,257,1]{2,1,0,3:T(8,128)S(1)} copy(f32[8,8,257,1]{3,1,2,0:T(8,128)} %broadcast_select_fusion.1) | data formatting | bytes 131584 | tf_op jit(solution)/shard_map/conv_general_dilated | solution.py:40
  248.1 5.3 %copy.109 = bf16[32,10,1,8,257]{0,3,4,1,2:T(8,128)(2,1)} copy(bf16[32,10,1,8,257]{4,3,0,1,2:T(8,128)(2,1)S(1)} %reshape.491) | data formatting | bytes 2631680 | tf_op jit(solution)/shard_map/conv_general_dilated | solution.py:40
  254.2 11.2 %fusion.14 = f32[8,8,257,32]{3,1,2,0:T(8,128)} fusion(bf16[32,32,3,3]{1,0,3,2:T(8,128)(2,1)S(1)} %copy-done, bf16[32,10,1,7,2]{0,3,4,1,2:T(8,128)(2,1)S(1)} %slice.1507, bf16[32,10,1,8,257]{0,3,4,1,2:T(8,128)(2,1)} %copy.109), kind=kOutput, calls=%fused_computation.13 | convolution fusion | flops 307147776 | bytes 3448576 | tf_op jit(solution)/shard_map/conv_general_dilated | solution.py:40
  265.4 7.3 %copy.110 = f32[8,8,257,32]{2,3,1,0:T(8,128)} copy(f32[8,8,257,32]{3,1,2,0:T(8,128)} %fusion.14) | data formatting | bytes 4210688 | tf_op jit(solution)/shard_map/conv_general_dilated | solution.py:40
  272.7 5.6 %multiply_convert_fusion.2 = (bf16[8,8,257,32]{2,3,1,0:T(8,128)(2,1)S(1)}, bf16[8,8,257,32]{2,3,1,0:T(8,128)(2,1)}, f32[8,8,257,32]{2,3,1,0:T(8,128)}) fusion(f32[8,8,257,32]{2,3,1,0:T(8,128)S(1)} %copy-done.2, pred[8,257]{1,0:T(8,128)(4,1)S(1)} %copy-done.79, f32[8,8,257,32]{2,3,1,0:T(8,128)} %copy.110), kind=kLoop, calls=%fused_computation.33 | loop fusion | flops 6842368 | bytes 8423432 | tf_op jit(solution)/shard_map/convert_element_type | solution.py:131
  278.9 2.0 reshape.465
  281.6 1.6 reshape.497
  287.5 3.4 copy.111
  290.9 4.3 reshape.495
  295.2 2.5 fusion.41
  297.8 5.5 %collective-permute-start.10 = (bf16[32,1,2048]{2,0,1:T(8,128)(2,1)S(1)}, bf16[32,1,2048]{2,0,1:T(8,128)(2,1)S(1)}, u32[]{:S(2)}, u32[]{:S(2)}) collective-permute-start(bf16[32,1,2048]{2,0,1:T(8,128)(2,1)S(1)} %get-tuple-element.51), channel_id=1, source_target_pairs={{0,1},{1,2},{2,3},{3,4},{4,5},{5,6},{6,7},{7,8},{8,9},{9,10},{10,1... | collective-permute-start | bytes 393224 | tf_op jit(solution)/shard_map/ppermute | solution.py:23
  307.2 2.5 reshape.500
  309.7 5.2 %copy.113 = bf16[32,10,1,8,257]{0,3,4,1,2:T(8,128)(2,1)} copy(bf16[32,10,1,8,257]{4,3,0,1,2:T(8,128)(2,1)S(1)} %reshape.500) | data formatting | bytes 2631680 | tf_op jit(solution)/shard_map/conv_general_dilated | solution.py:40
  315.7 11.8 %broadcast_select_fusion = f32[8,8,257,1]{3,1,2,0:T(8,128)} fusion(pred[8,257]{0,1:T(8,128)(4,1)S(1)} %copy-done.83, bf16[32,10,1,7,2]{0,3,4,1,2:T(8,128)(2,1)S(1)} %slice.1511, bf16[32,10,1,8,257]{0,3,4,1,2:T(8,128)(2,1)} %copy.113, bf16[1,32,3,3]{1,3,2,0:T(4,128)(2,1)S(1)} %bitcast.470), kind=kOutput, calls=%fused_computation.29 | convolution fusion | flops 13468736 | bytes 1393224 | tf_op jit(solution)/shard_map/conv_general_dilated | solution.py:40
  327.5 6.3 %copy.115 = f32[8,8,257,1]{2,1,0,3:T(8,128)S(1)} copy(f32[8,8,257,1]{3,1,2,0:T(8,128)} %broadcast_select_fusion) | data formatting | bytes 131584 | tf_op jit(solution)/shard_map/conv_general_dilated | solution.py:40
  339.2 8.8 %all-to-all-start.2 = ((f32[8,16,128]{2,0,1:T(8,128)}), f32[8,16,128]{2,0,1:T(8,128)S(1)}, u32[]{:S(2)}, u32[]{:S(2)}) async-start(f32[8,16,128]{2,0,1:T(8,128)} %add_bitcast_fusion), calls=%async_computation.2 | async-start | bytes 131072 | tf_op jit(solution)/shard_map/all_to_all | solution.py:114
  350.7 4.3 all-to-all-done.2
  354.9 15.9 %broadcast_multiply_fusion.46 = (f32[128,128]{1,0:T(8,128)S(1)}, f32[128,128]{1,0:T(8,128)S(1)}) fusion(f32[]{:T(128)} %bitcast.9, f32[]{:T(128)} %bitcast.61, f32[]{:T(128)} %bitcast.60, f32[]{:T(128)} %bitcast.59, f32[]{:T(128)} %bitcast.58, f32[]{:T(128)} %bitcast.57, f32[]{:T(128)} %bitcast.56, f32[]{:T(128)} %bitcast.55, f32[]{:T(128)} %bitcast.54, ...), kind=kLoop, calls=%fused_computation.671 | loop fusion | flops 819200 | bytes 196708 | tf_op jit(solution)/shard_map/mul | solution.py:82
  370.8 3.3 broadcast_multiply_fusion.42
  374.1 11.4 %broadcast_multiply_fusion.44 = (f32[128,128]{1,0:T(8,128)S(1)}, f32[128,128]{1,0:T(8,128)S(1)}, f32[128,128]{1,0:T(8,128)S(1)}, f32[128,128]{1,0:T(8,128)S(1)},...) fusion(f32[128,128]{1,0:T(8,128)S(1)} %get-tuple-element.36, ...), kind=kLoop, calls=%fused_computation.669 | loop fusion | flops 294912 | bytes 1245256 | tf_op jit(solution)/shard_map/mul | solution.py:82
  385.6 1.4 fusion.341
  387.0 3.5 all-to-all-start.3
  390.6 64.1 %all-reduce.103 = (f32[32,1,3,3]{0,1,3,2:T(1,128)}, f32[32,32,3,3]{1,0,3,2:T(8,128)}, f32[1,32,3,3]{1,0,3,2:T(1,128)}) all-reduce(f32[32,1,3,3]{0,1,3,2:T(1,128)S(1)} %maximum_multiply_fusion.1, f32[32,32,3,3]{1,0,3,2:T(8,128)S(1)} %copy-done.14, ...), channel_id=1, replica_groups=mesh['parts'=2,'rows'=16] {'rows'}, use_global_device_ids=true, to_apply=%region_1.2 | all-reduce | flops 9792 | bytes 78336 | tf_op jit(solution)/shard_map/psum | solution.py:169
  (300 shorter events, 55.2 us)
Async XLA Ops:
  0.6 139.3 %copy-start = (bf16[32,32,3,3]{1,0,3,2:T(8,128)(2,1)S(1)}, bf16[32,32,3,3]{1,0,3,2:T(8,128)(2,1)}, u32[]{:S(2)}) copy-start(bf16[32,32,3,3]{1,0,3,2:T(8,128)(2,1)} %param.16) | copy-start | bytes 55300
  1.5 64.8 %collective-permute-start.6 = (bf16[1,1,2048]{2,1,0:T(2,128)(2,1)S(1)}, bf16[1,1,2048]{2,1,0:T(2,128)(2,1)S(1)}, u32[]{:S(2)}, u32[]{:S(2)}) collective-permute-start(bf16[1,1,2048]{2,1,0:T(2,128)(2,1)S(1)} %get-tuple-element.165), channel_id=1, source_target_pairs={{0,1},{1,2},{2,3},{3,4},{4,5},{5,6},{6,7},{7,8},{8,9},{9,10},{10,1... | collective-permute-start | bytes 12296 | tf_op jit(solution)/shard_map/ppermute | solution.py:23
  3.9 62.4 %collective-permute-start.7 = (bf16[1,1,2048]{2,1,0:T(2,128)(2,1)S(1)}, bf16[1,1,2048]{2,1,0:T(2,128)(2,1)S(1)}, u32[]{:S(2)}, u32[]{:S(2)}) collective-permute-start(bf16[1,1,2048]{2,1,0:T(2,128)(2,1)S(1)} %get-tuple-element.166), channel_id=1, source_target_pairs={{1,0},{2,1},{3,2},{4,3},{5,4},{6,5},{7,6},{8,7},{9,8},{10,9},{11,1... | collective-permute-start | bytes 12296 | tf_op jit(solution)/shard_map/ppermute | solution.py:24
  8.6 64.7 %copy-start.17 = (f32[2048]{0:T(1024)}, f32[2048]{0:T(1024)S(1)}, u32[]{:S(2)}) copy-start(f32[2048]{0:T(1024)S(1)} %broadcast_bitcast_fusion.24) | copy-start | bytes 24580
  8.7 64.6 %copy-start.19 = (f32[2048]{0:T(1024)}, f32[2048]{0:T(1024)S(1)}, u32[]{:S(2)}) copy-start(f32[2048]{0:T(1024)S(1)} %get-tuple-element.216) | copy-start | bytes 24580
  8.7 64.6 %copy-start.21 = (f32[2048]{0:T(1024)}, f32[2048]{0:T(1024)S(1)}, u32[]{:S(2)}) copy-start(f32[2048]{0:T(1024)S(1)} %get-tuple-element.217) | copy-start | bytes 24580
  8.7 64.5 %copy-start.39 = (f32[2048]{0:T(1024)}, f32[2048]{0:T(1024)S(1)}, u32[]{:S(2)}) copy-start(f32[2048]{0:T(1024)S(1)} %get-tuple-element.194) | copy-start | bytes 24580
  8.7 64.5 %copy-start.41 = (f32[2048]{0:T(1024)}, f32[2048]{0:T(1024)S(1)}, u32[]{:S(2)}) copy-start(f32[2048]{0:T(1024)S(1)} %get-tuple-element.195) | copy-start | bytes 24580
  8.8 64.4 %copy-start.47 = (f32[2048]{0:T(1024)}, f32[2048]{0:T(1024)S(1)}, u32[]{:S(2)}) copy-start(f32[2048]{0:T(1024)S(1)} %get-tuple-element.196) | copy-start | bytes 24580
  8.8 64.4 %copy-start.49 = (f32[2048]{0:T(1024)}, f32[2048]{0:T(1024)S(1)}, u32[]{:S(2)}) copy-start(f32[2048]{0:T(1024)S(1)} %get-tuple-element.197) | copy-start | bytes 24580
  8.9 64.3 %copy-start.55 = (f32[2048]{0:T(1024)}, f32[2048]{0:T(1024)S(1)}, u32[]{:S(2)}) copy-start(f32[2048]{0:T(1024)S(1)} %get-tuple-element.198) | copy-start | bytes 24580
  8.9 64.3 %copy-start.57 = (f32[2048]{0:T(1024)}, f32[2048]{0:T(1024)S(1)}, u32[]{:S(2)}) copy-start(f32[2048]{0:T(1024)S(1)} %get-tuple-element.199) | copy-start | bytes 24580
  9.0 64.4 %copy-start.25 = (f32[2048]{0:T(1024)}, f32[2048]{0:T(1024)S(1)}, u32[]{:S(2)}) copy-start(f32[2048]{0:T(1024)S(1)} %get-tuple-element.200) | copy-start | bytes 24580
  9.0 64.4 %copy-start.27 = (f32[2048]{0:T(1024)}, f32[2048]{0:T(1024)S(1)}, u32[]{:S(2)}) copy-start(f32[2048]{0:T(1024)S(1)} %get-tuple-element.201) | copy-start | bytes 24580
  9.0 64.3 %copy-start.29 = (f32[2048]{0:T(1024)}, f32[2048]{0:T(1024)S(1)}, u32[]{:S(2)}) copy-start(f32[2048]{0:T(1024)S(1)} %get-tuple-element.202) | copy-start | bytes 24580
  9.0 64.3 %copy-start.31 = (f32[2048]{0:T(1024)}, f32[2048]{0:T(1024)S(1)}, u32[]{:S(2)}) copy-start(f32[2048]{0:T(1024)S(1)} %get-tuple-element.203) | copy-start | bytes 24580
  9.1 64.2 %copy-start.33 = (f32[2048]{0:T(1024)}, f32[2048]{0:T(1024)S(1)}, u32[]{:S(2)}) copy-start(f32[2048]{0:T(1024)S(1)} %get-tuple-element.204) | copy-start | bytes 24580
  9.1 64.3 %copy-start.35 = (f32[2048]{0:T(1024)}, f32[2048]{0:T(1024)S(1)}, u32[]{:S(2)}) copy-start(f32[2048]{0:T(1024)S(1)} %get-tuple-element.205) | copy-start | bytes 24580
  9.2 64.2 %copy-start.37 = (f32[2048]{0:T(1024)}, f32[2048]{0:T(1024)S(1)}, u32[]{:S(2)}) copy-start(f32[2048]{0:T(1024)S(1)} %get-tuple-element.207) | copy-start | bytes 24580
  9.2 64.4 %copy-start.23 = (f32[2048]{0:T(1024)}, f32[2048]{0:T(1024)S(1)}, u32[]{:S(2)}) copy-start(f32[2048]{0:T(1024)S(1)} %get-tuple-element.206) | copy-start | bytes 24580
  9.3 64.1 %copy-start.43 = (f32[2048]{0:T(1024)}, f32[2048]{0:T(1024)S(1)}, u32[]{:S(2)}) copy-start(f32[2048]{0:T(1024)S(1)} %get-tuple-element.208) | copy-start | bytes 24580
  9.3 64.1 %copy-start.45 = (f32[2048]{0:T(1024)}, f32[2048]{0:T(1024)S(1)}, u32[]{:S(2)}) copy-start(f32[2048]{0:T(1024)S(1)} %get-tuple-element.209) | copy-start | bytes 24580
  9.3 64.1 %copy-start.51 = (f32[2048]{0:T(1024)}, f32[2048]{0:T(1024)S(1)}, u32[]{:S(2)}) copy-start(f32[2048]{0:T(1024)S(1)} %get-tuple-element.210) | copy-start | bytes 24580
  9.3 64.1 %copy-start.53 = (f32[2048]{0:T(1024)}, f32[2048]{0:T(1024)S(1)}, u32[]{:S(2)}) copy-start(f32[2048]{0:T(1024)S(1)} %get-tuple-element.211) | copy-start | bytes 24580
  9.4 64.0 %copy-start.59 = (f32[2048]{0:T(1024)}, f32[2048]{0:T(1024)S(1)}, u32[]{:S(2)}) copy-start(f32[2048]{0:T(1024)S(1)} %get-tuple-element.212) | copy-start | bytes 24580
  9.4 64.0 %copy-start.61 = (f32[2048]{0:T(1024)}, f32[2048]{0:T(1024)S(1)}, u32[]{:S(2)}) copy-start(f32[2048]{0:T(1024)S(1)} %get-tuple-element.213) | copy-start | bytes 24580
  9.5 64.0 %copy-start.63 = (f32[2048]{0:T(1024)}, f32[2048]{0:T(1024)S(1)}, u32[]{:S(2)}) copy-start(f32[2048]{0:T(1024)S(1)} %get-tuple-element.214) | copy-start | bytes 24580
  9.5 64.0 %copy-start.65 = (f32[2048]{0:T(1024)}, f32[2048]{0:T(1024)S(1)}, u32[]{:S(2)}) copy-start(f32[2048]{0:T(1024)S(1)} %get-tuple-element.215) | copy-start | bytes 24580
  13.1 16.2 %all-to-all-start = ((f32[8,16,128]{2,0,1:T(8,128)}), f32[8,16,128]{2,0,1:T(8,128)S(1)}, u32[]{:S(2)}, u32[]{:S(2)}) async-start(f32[8,16,128]{2,0,1:T(8,128)} %add_bitcast_fusion.1), calls=%async_computation | async-start | bytes 131072 | tf_op jit(solution)/shard_map/all_to_all | solution.py:114
  62.2 11.4 %copy-start.15 = (f32[8,2048]{1,0:T(8,128)S(1)}, f32[8,2048]{1,0:T(8,128)}, u32[]{:S(2)}) copy-start(f32[8,2048]{1,0:T(8,128)} %param.9) | copy-start | bytes 196612
  62.2 11.0 %all-to-all-start.1 = ((f32[16,8,128]{2,1,0:T(8,128)}), f32[16,8,128]{2,1,0:T(8,128)S(1)}, u32[]{:S(2)}, u32[]{:S(2)}) async-start(f32[16,8,128]{2,1,0:T(8,128)} %fusion.342), calls=%async_computation.1 | async-start | bytes 131072 | tf_op jit(solution)/shard_map/all_to_all | solution.py:119
  74.8 17.7 %collective-permute-start = (bf16[1,1,2048]{2,1,0:T(2,128)(2,1)S(1)}, bf16[1,1,2048]{2,1,0:T(2,128)(2,1)S(1)}, u32[]{:S(2)}, u32[]{:S(2)}) collective-permute-start(bf16[1,1,2048]{2,1,0:T(2,128)(2,1)S(1)} %get-tuple-element.167), channel_id=1, source_target_pairs={{0,1},{1,2},{2,3},{3,4},{4,5},{5,6},{6,7},{7,8},{8,9},{9,10},{10,1... | collective-permute-start | bytes 12296 | tf_op jit(solution)/shard_map/ppermute | solution.py:23
  76.2 16.2 %collective-permute-start.1 = (bf16[1,1,2048]{2,1,0:T(2,128)(2,1)S(1)}, bf16[1,1,2048]{2,1,0:T(2,128)(2,1)S(1)}, u32[]{:S(2)}, u32[]{:S(2)}) collective-permute-start(bf16[1,1,2048]{2,1,0:T(2,128)(2,1)S(1)} %get-tuple-element.168), channel_id=1, source_target_pairs={{1,0},{2,1},{3,2},{4,3},{5,4},{6,5},{7,6},{8,7},{9,8},{10,9},{11,1... | collective-permute-start | bytes 12296 | tf_op jit(solution)/shard_map/ppermute | solution.py:24
  92.5 2.4 copy-start.80
  102.5 5.9 %copy-start.79 = (pred[8,257]{1,0:T(8,128)(4,1)S(1)}, pred[8,257]{1,0:T(8,128)(4,1)}, u32[]{:S(2)}) copy-start(pred[8,257]{1,0:T(8,128)(4,1)} %constant.281) | copy-start | bytes 6172
  116.4 5.8 %copy-start.3 = (f32[8,1,2056,32]{2,3,0,1:T(8,128)}, f32[8,1,2056,32]{2,3,0,1:T(8,128)S(1)}, u32[]{:S(2)}) copy-start(f32[8,1,2056,32]{2,3,0,1:T(8,128)S(1)} %reshape.463) | copy-start | bytes 6316036
  117.0 7.9 %copy-start.8 = (bf16[32,8,2048]{2,0,1:T(8,128)(2,1)}, bf16[32,8,2048]{2,0,1:T(8,128)(2,1)S(1)}, u32[]{:S(2)}) copy-start(bf16[32,8,2048]{2,0,1:T(8,128)(2,1)S(1)} %multiply_convert_fusion.4) | copy-start | bytes 3145732
  117.0 5.2 %collective-permute-start.2 = (bf16[32,1,2048]{2,0,1:T(8,128)(2,1)S(1)}, bf16[32,1,2048]{2,0,1:T(8,128)(2,1)S(1)}, u32[]{:S(2)}, u32[]{:S(2)}) collective-permute-start(bf16[32,1,2048]{2,0,1:T(8,128)(2,1)S(1)} %get-tuple-element.57), channel_id=1, source_target_pairs={{0,1},{1,2},{2,3},{3,4},{4,5},{5,6},{6,7},{7,8},{8,9},{9,10},{10,1... | collective-permute-start | bytes 393224 | tf_op jit(solution)/shard_map/ppermute | solution.py:23
  120.3 4.5 collective-permute-start.3
  194.2 15.1 %copy-start.9 = (bf16[32,8,2048]{2,0,1:T(8,128)(2,1)S(1)}, bf16[32,8,2048]{2,0,1:T(8,128)(2,1)}, u32[]{:S(2)}) copy-start(bf16[32,8,2048]{2,0,1:T(8,128)(2,1)} %copy-done.8) | copy-start | bytes 3145732
  196.0 18.7 %collective-permute-start.4 = (bf16[32,1,2048]{2,0,1:T(8,128)(2,1)}, bf16[32,1,2048]{2,0,1:T(8,128)(2,1)}, u32[]{:S(2)}, u32[]{:S(2)}) collective-permute-start(bf16[32,1,2048]{2,0,1:T(8,128)(2,1)} %get-tuple-element.55), channel_id=1, source_target_pairs={{0,1},{1,2},{2,3},{3,4},{4,5},{5,6},{6,7},{7,8},{8,9},{9,10},{10,1... | collective-permute-start | bytes 393224 | tf_op jit(solution)/shard_map/ppermute | solution.py:23
  202.1 12.6 %collective-permute-start.5 = (bf16[32,1,2048]{2,0,1:T(8,128)(2,1)}, bf16[32,1,2048]{2,0,1:T(8,128)(2,1)}, u32[]{:S(2)}, u32[]{:S(2)}) collective-permute-start(bf16[32,1,2048]{2,0,1:T(8,128)(2,1)} %get-tuple-element.56), channel_id=1, source_target_pairs={{1,0},{2,1},{3,2},{4,3},{5,4},{6,5},{7,6},{8,7},{9,8},{10,9},{11,1... | collective-permute-start | bytes 393224 | tf_op jit(solution)/shard_map/ppermute | solution.py:24
  203.4 7.0 %collective-permute-start.8 = (bf16[32,1,2048]{2,0,1:T(8,128)(2,1)}, bf16[32,1,2048]{2,0,1:T(8,128)(2,1)S(1)}, u32[]{:S(2)}, u32[]{:S(2)}) collective-permute-start(bf16[32,1,2048]{2,0,1:T(8,128)(2,1)} %get-tuple-element.53), channel_id=1, source_target_pairs={{0,1},{1,2},{2,3},{3,4},{4,5},{5,6},{6,7},{7,8},{8,9},{9,10},{10,1... | collective-permute-start | bytes 393224 | tf_op jit(solution)/shard_map/ppermute | solution.py:23
  206.4 5.0 %collective-permute-start.9 = (bf16[32,1,2048]{2,0,1:T(8,128)(2,1)S(1)}, bf16[32,1,2048]{2,0,1:T(8,128)(2,1)S(1)}, u32[]{:S(2)}, u32[]{:S(2)}) collective-permute-start(bf16[32,1,2048]{2,0,1:T(8,128)(2,1)S(1)} %get-tuple-element.54), channel_id=1, source_target_pairs={{1,0},{2,1},{3,2},{4,3},{5,4},{6,5},{7,6},{8,7},{9,8},{10,9},{11,1... | collective-permute-start | bytes 393224 | tf_op jit(solution)/shard_map/ppermute | solution.py:24
  221.1 8.4 %copy-start.81 = (bf16[1,32,3,3]{1,3,2,0:T(4,128)(2,1)S(1)}, bf16[1,32,3,3]{1,3,2,0:T(4,128)(2,1)}, u32[]{:S(2)}) copy-start(bf16[1,32,3,3]{1,3,2,0:T(4,128)(2,1)} %param.17) | copy-start | bytes 1732
  221.1 8.4 %copy-start.82 = (pred[8,257]{0,1:T(8,128)(4,1)S(1)}, pred[8,257]{0,1:T(8,128)(4,1)}, u32[]{:S(2)}) copy-start(pred[8,257]{0,1:T(8,128)(4,1)} %constant.287) | copy-start | bytes 6172
  265.4 7.3 %copy-start.2 = (f32[8,8,257,32]{2,3,1,0:T(8,128)S(1)}, f32[8,8,257,32]{2,3,1,0:T(8,128)}, u32[]{:S(2)}) copy-start(f32[8,8,257,32]{2,3,1,0:T(8,128)} %copy-done.1) | copy-start | bytes 6316036
  278.9 2.0 copy-start.7
  281.6 2.0 copy-start.78
  290.9 4.3 copy-start.4
  295.2 9.3 %copy-start.12 = (bf16[8,1,2056,32]{2,3,0,1:T(8,128)(2,1)S(1)}, bf16[8,1,2056,32]{2,3,0,1:T(8,128)(2,1)}, u32[]{:S(2)}) copy-start(bf16[8,1,2056,32]{2,3,0,1:T(8,128)(2,1)} %reshape.488) | copy-start | bytes 3158020
  295.2 9.3 %copy-start.13 = (bf16[8,1,2056,32]{2,3,0,1:T(8,128)(2,1)S(1)}, bf16[8,1,2056,32]{2,3,0,1:T(8,128)(2,1)}, u32[]{:S(2)}) copy-start(bf16[8,1,2056,32]{2,3,0,1:T(8,128)(2,1)} %reshape.465) | copy-start | bytes 3158020
  297.7 7.2 %copy-start.68 = (f32[32,32,1]{1,0,2:T(8,128)S(1)}, f32[32,32,1]{1,0,2:T(8,128)}, u32[]{:S(2)}) copy-start(f32[32,32,1]{1,0,2:T(8,128)} %fusion.73) | copy-start | bytes 12292
  297.7 7.2 %copy-start.69 = (f32[32,32,1]{1,0,2:T(8,128)S(1)}, f32[32,32,1]{1,0,2:T(8,128)}, u32[]{:S(2)}) copy-start(f32[32,32,1]{1,0,2:T(8,128)} %fusion.75) | copy-start | bytes 12292
  297.7 7.3 %copy-start.67 = (f32[32,32,1,3]{1,0,3,2:T(8,128)S(1)}, f32[32,32,1,3]{1,0,3,2:T(8,128)}, u32[]{:S(2)}) copy-start(f32[32,32,1,3]{1,0,3,2:T(8,128)} %maximum_bitcast_fusion.3) | copy-start | bytes 36868
  297.8 7.9 %collective-permute-start.10 = (bf16[32,1,2048]{2,0,1:T(8,128)(2,1)S(1)}, bf16[32,1,2048]{2,0,1:T(8,128)(2,1)S(1)}, u32[]{:S(2)}, u32[]{:S(2)}) collective-permute-start(bf16[32,1,2048]{2,0,1:T(8,128)(2,1)S(1)} %get-tuple-element.51), channel_id=1, source_target_pairs={{0,1},{1,2},{2,3},{3,4},{4,5},{5,6},{6,7},{7,8},{8,9},{9,10},{10,1... | collective-permute-start | bytes 393224 | tf_op jit(solution)/shard_map/ppermute | solution.py:23
  303.2 3.2 collective-permute-start.11
  309.7 6.0 %copy-start.83 = (pred[8,257]{0,1:T(8,128)(4,1)S(1)}, pred[8,257]{0,1:T(8,128)(4,1)}, u32[]{:S(2)}) copy-start(pred[8,257]{0,1:T(8,128)(4,1)} %constant.287) | copy-start | bytes 6172
  327.5 6.4 %copy-start.16 = (f32[8,2048]{1,0:T(8,128)S(1)}, f32[8,2048]{1,0:T(8,128)}, u32[]{:S(2)}) copy-start(f32[8,2048]{1,0:T(8,128)} %param.11) | copy-start | bytes 196612
  327.5 6.4 %copy-start.10 = (bf16[32,8,2048]{2,0,1:T(8,128)(2,1)S(1)}, bf16[32,8,2048]{2,0,1:T(8,128)(2,1)}, u32[]{:S(2)}) copy-start(bf16[32,8,2048]{2,0,1:T(8,128)(2,1)} %get-tuple-element.46) | copy-start | bytes 3145732
  327.5 6.8 %copy-start.11 = (bf16[32,10,2048]{2,0,1:T(8,128)(2,1)S(1)}, bf16[32,10,2048]{2,0,1:T(8,128)(2,1)}, u32[]{:S(2)}) copy-start(bf16[32,10,2048]{2,0,1:T(8,128)(2,1)} %get-tuple-element.47) | copy-start | bytes 3932164
  339.2 15.7 %all-to-all-start.2 = ((f32[8,16,128]{2,0,1:T(8,128)}), f32[8,16,128]{2,0,1:T(8,128)S(1)}, u32[]{:S(2)}, u32[]{:S(2)}) async-start(f32[8,16,128]{2,0,1:T(8,128)} %add_bitcast_fusion), calls=%async_computation.2 | async-start | bytes 131072 | tf_op jit(solution)/shard_map/all_to_all | solution.py:114
  350.6 39.9 %copy-start.14 = (f32[32,32,3,3]{1,0,3,2:T(8,128)S(1)}, f32[32,32,3,3]{1,0,3,2:T(8,128)}, u32[]{:S(2)}) copy-start(f32[32,32,3,3]{1,0,3,2:T(8,128)} %maximum_multiply_fusion) | copy-start | bytes 110596
  387.0 67.7 %all-to-all-start.3 = ((f32[16,8,128]{2,1,0:T(8,128)}), f32[16,8,128]{2,1,0:T(8,128)S(1)}, u32[]{:S(2)}, u32[]{:S(2)}) async-start(f32[16,8,128]{2,1,0:T(8,128)} %fusion.341), calls=%async_computation.3 | async-start | bytes 131072 | tf_op jit(solution)/shard_map/all_to_all | solution.py:119
  (36 other events, 62.0 us)
where the time goes:
time: 463 us; the launch traced here: 456 us
  local copies, waits for them, and re-layouts  139 us (30%)
  other arithmetic  99.6 us (22%)
  matrix products  80.2 us (17%)
  blocking collectives  64.1 us (14%)
  starting transfers between devices  55.3 us (12%)
  waiting for transfers between devices  15.9 us (3%)
    conv_general_dilated x34, local copies, waits for them, and re-layouts, conv_rim(): lax.conv_general_dilated(padded[None], weight, (1, 1), padding, dimension...  116 us
    psum x1, blocking collectives, on_device(): lax.psum((partial_grads[0] * grad_scale, partial_grads[1] * grad_scale, p...  64.1 us
    mul x10, other arithmetic, blur_line(): spread = jnp.pad(factor * values, widths)  62.5 us
    conv_general_dilated x6, matrix products, conv_rim(): lax.conv_general_dilated(padded[None], weight, (1, 1), padding, dimension...  61 us
    ppermute x6, starting transfers between devices, padded_2(): before = lax.ppermute(last, axis, up)  21.6 us
    all_to_all x2, starting transfers between devices, data_gradient(): lax.all_to_all(blurred, 'rows', split_axis=1, concat_axis=0, tiled=True)  18.1 us
    dot_general x27, matrix products, weight_taps(): jnp.einsum('ohw,chw->oc', errors, window, preferred_element_type=jnp.floa...  16.8 us
    convert_element_type x2, other arithmetic, denoise(): (conv_rim(cot_pad, flipped(w_last)) * silu_slope(pre_mid)).astype(jnp.bfl...  10.5 us
  transfers between devices with their start and end apart: 16, of which 6 were waited for; matrix products, arithmetic and copies ran while one was open for 16% of the time, Pallas kernels for 0%

commit v1 on v0

v1 whole, which is shorter than its diff:
```python
import functools
import math

import jax
import jax.numpy as jnp
import numpy as np
from jax import lax
from jax.experimental import pallas as pl
from jax.experimental.pallas import tpu as pltpu
from jax.sharding import PartitionSpec as P

BLK = 128
RAD = 12
TAPS = 2 * RAD + 1
CH = 32
BAND = 8
STEP_SIZE = 2.0
GRAD_FACTOR = 8.0
MESH = pl.DeviceIdType.MESH
F32 = jnp.float32
BF16 = jnp.bfloat16

EXT_ROWS = list(range(8)) + [-4, -3, -2, -1, 8, 9, 10, 11]


def band_select(out_rows, in_rows, sign):
    table = np.zeros((len(out_rows), len(in_rows), 3), np.float32)
    for i, r in enumerate(out_rows):
        for j, q in enumerate(in_rows):
            a = sign * (q - r) + 1
            if 0 <= a <= 2:
                table[i, j, a] = 1.0
    return table


ROWS_14 = list(range(-3, 11))
ROWS_12 = list(range(-2, 10))
ROWS_10 = list(range(-1, 9))
ROWS_8 = list(range(8))


def silu_pair(v):
    s = 1.0 / (1.0 + jnp.exp(-v))
    return v * s, s * (1.0 + v * (1.0 - s))


def shifted(v, delta):
    width = v.shape[1]
    lane = lax.broadcasted_iota(jnp.int32, v.shape, 1)
    if delta == 1:
        return jnp.where(lane < width - 1, pltpu.roll(v, width - 1, 1), 0.0)
    return jnp.where(lane > 0, pltpu.roll(v, 1, 1), 0.0)


def nt_dot(a, b):
    return lax.dot_general(a, b, (((1,), (1,)), ((), ())), preferred_element_type=F32)


def denoise_kernel(
    n, scale,
    ds_ref, cot_ref, w1_ref, wm_ref, wl_ref, wlt_ref, wmt_ref, wf_ref,
    den_ref, gd_ref, pg_ref,
    wmb, wmtb, f3, c3, pre1, x3, pm, z3, bfr, d24, gm_acc, gf_acc, gl_acc,
):
    me = lax.axis_index("rows")
    width = ds_ref.shape[1]
    step = 512 if width % 512 == 0 else 128
    chunks = width // step
    first, last = me == 0, me == n - 1

    def valid(row):
        below = jnp.logical_and(row < 0, first)
        above = jnp.logical_and(row >= BAND, last)
        return jnp.logical_not(jnp.logical_or(below, above))

    wmb[...] = jnp.zeros_like(wmb)
    wmtb[...] = jnp.zeros_like(wmtb)
    for b in range(3):
        for r in range(12):
            wmb[r * 32 : r * 32 + 32, b * 448 + r * 32 : b * 448 + r * 32 + 96] = wm_ref[:, b * 96 : b * 96 + 96]
        for r in range(10):
            wmtb[r * 32 : r * 32 + 32, b * 384 + r * 32 : b * 384 + r * 32 + 96] = wmt_ref[:, b * 96 : b * 96 + 96]

    sub = lax.broadcasted_iota(jnp.int32, (16, width), 0)
    outside = jnp.logical_or(
        jnp.logical_and(jnp.logical_and(sub >= 8, sub < 12), first),
        jnp.logical_and(sub >= 12, last),
    )
    ds = jnp.where(outside, 0.0, ds_ref[...])
    cot = jnp.where(outside, 0.0, cot_ref[...])
    f3[0:16, :] = shifted(ds, -1).astype(BF16)
    f3[16:32, :] = ds.astype(BF16)
    f3[32:48, :] = shifted(ds, 1).astype(BF16)
    c3[0:16, :] = shifted(cot, 1).astype(BF16)
    c3[16:32, :] = cot.astype(BF16)
    c3[32:48, :] = shifted(cot, -1).astype(BF16)

    def at(i):
        return pl.ds(pl.multiple_of(i * step, step), step)

    def grp(i):
        return pl.ds(pl.multiple_of(i * 32, 32), 32)

    @pl.loop(0, chunks)
    def _(i):
        pre1[:, at(i)] = jnp.dot(w1_ref[...], f3[:, at(i)], preferred_element_type=F32).astype(pre1.dtype)

    @pl.loop(0, 14)
    def _(r):
        act, slope = silu_pair(pre1[grp(r), :].astype(F32))
        act = jnp.where(valid(r - 3), act, 0.0)
        pre1[grp(r), :] = slope.astype(pre1.dtype)
        x3[grp(r), :] = shifted(act, -1).astype(BF16)
        x3[grp(r + 14), :] = act.astype(BF16)
        x3[grp(r + 28), :] = shifted(act, 1).astype(BF16)

    @pl.loop(0, chunks)
    def _(i):
        pm[:, at(i)] = jnp.dot(wmb[...], x3[:, at(i)], preferred_element_type=F32).astype(pm.dtype)

    @pl.loop(0, 12)
    def _(r):
        act, slope = silu_pair(pm[grp(r), :].astype(F32))
        act = jnp.where(valid(r - 2), act, 0.0)
        slope = jnp.where(valid(r - 2), slope, 0.0)
        pm[grp(r), :] = slope.astype(pm.dtype)
        z3[grp(r), :] = act.astype(BF16)

    gl_acc[...] = jnp.zeros_like(gl_acc)

    @pl.loop(0, chunks)
    def _(i):
        part = z3[32:352, at(i)]
        d24[:, at(i)] = jnp.dot(wl_ref[...], part, preferred_element_type=F32)
        gl_acc[...] += nt_dot(c3[:, at(i)], part)
        back = pm[:, at(i)].astype(F32) * jnp.dot(wlt_ref[...], c3[:, at(i)], preferred_element_type=F32)
        pm[:, at(i)] = back.astype(pm.dtype)

    den_ref[...] = ds_ref[0:8, :] + d24[8:16, :] + shifted(d24[0:8, :], -1) + shifted(d24[16:24, :], 1)

    @pl.loop(0, 12)
    def _(r):
        back = pm[grp(r), :].astype(F32)
        z3[grp(r), :] = shifted(back, 1).astype(BF16)
        z3[grp(r + 12), :] = back.astype(BF16)
        z3[grp(r + 24), :] = shifted(back, -1).astype(BF16)

    gm_acc[...] = jnp.zeros_like(gm_acc)
    gf_acc[...] = jnp.zeros_like(gf_acc)
    row = lax.broadcasted_iota(jnp.int32, (320, step), 0)
    gone = jnp.logical_or(jnp.logical_and(row < 32, first), jnp.logical_and(row >= 288, last))

    @pl.loop(0, chunks)
    def _(i):
        back = jnp.dot(wmtb[...], z3[:, at(i)], preferred_element_type=F32) * pre1[64:384, at(i)].astype(F32)
        back = jnp.where(gone, 0.0, back).astype(BF16)
        bfr[...] = back
        d24[:, at(i)] = jnp.dot(wf_ref[...], back, preferred_element_type=F32)
        gf_acc[...] += nt_dot(bfr[32:288, :], f3[:, at(i)])
        errors = z3[384 + 64 : 384 + 320, at(i)]
        for b in range(3):
            gm_acc[b] += nt_dot(errors, x3[b * 448 + 64 : b * 448 + 384, at(i)])

    gd_ref[...] = cot_ref[0:8, :] + d24[8:16, :] + shifted(d24[0:8, :], 1) + shifted(d24[16:24, :], -1)

    pg_ref[...] = jnp.zeros_like(pg_ref)
    for a in range(3):
        for b in range(3):
            total = gm_acc[b, 0:32, a * 32 : a * 32 + 32]
            for r in range(1, 8):
                total = total + gm_acc[b, r * 32 : r * 32 + 32, (r + a) * 32 : (r + a) * 32 + 32]
            slot = a * 3 + b
            pg_ref[slot // 4 * 32 : slot // 4 * 32 + 32, slot % 4 * 32 : slot % 4 * 32 + 32] = total * scale
            total_first = jnp.zeros((32, 1), F32)
            total_last = jnp.zeros((1, 32), F32)
            for r in range(8):
                col = b * 16 + EXT_ROWS.index(r + a - 1)
                total_first = total_first + gf_acc[r * 32 : r * 32 + 32, col : col + 1]
                total_last = total_last + gl_acc[b * 16 + r : b * 16 + r + 1, (r + a) * 32 : (r + a) * 32 + 32]
            pg_ref[64:96, 32 + slot : 33 + slot] = total_first * scale
            pg_ref[64 + slot : 65 + slot, 64:96] = total_last * scale


def denoise(n, scale, ds_ext, cot_ext, w_first, w_mid, w_last):
    width = ds_ext.shape[1]
    keep = F32 if width <= 4096 else BF16
    wf, wl = w_first[:, 0], w_last[0]

    def ein(spec, table, weight, shape):
        return jnp.einsum(spec, jnp.asarray(table, BF16), weight, preferred_element_type=F32).astype(BF16).reshape(shape)

    w1 = ein("rea,oab->robe", band_select(ROWS_14, EXT_ROWS, 1), wf, (448, 48))
    wl3 = ein("rea,cab->brec", band_select(ROWS_8, ROWS_10, 1), wl, (24, 320))
    wlt = ein("rea,cab->rcbe", band_select(ROWS_12, EXT_ROWS, -1), wl, (384, 48))
    wf3 = ein("rea,oab->breo", band_select(ROWS_8, ROWS_10, -1), wf, (24, 320))
    wm = jnp.transpose(w_mid, (0, 3, 2, 1)).reshape(32, 288)
    wmt = jnp.transpose(jnp.flip(w_mid, 2), (1, 3, 2, 0)).reshape(32, 288)
    return pl.pallas_call(
        functools.partial(denoise_kernel, n, scale),
        out_shape=(
            jax.ShapeDtypeStruct((8, width), F32),
            jax.ShapeDtypeStruct((8, width), F32),
            jax.ShapeDtypeStruct((8 * n, 128), F32),
        ),
        in_specs=[pl.BlockSpec(memory_space=pltpu.VMEM)] * 8,
        out_specs=[pl.BlockSpec(memory_space=pltpu.VMEM)] * 3,
        scratch_shapes=[
            pltpu.VMEM((384, 1344), BF16),
            pltpu.VMEM((320, 1152), BF16),
            pltpu.VMEM((48, width), BF16),
            pltpu.VMEM((48, width), BF16),
            pltpu.VMEM((448, width), keep),
            pltpu.VMEM((1344, width), BF16),
            pltpu.VMEM((384, width), keep),
            pltpu.VMEM((1152, width), BF16),
            pltpu.VMEM((320, 512 if width % 512 == 0 else 128), BF16),
            pltpu.VMEM((24, width), F32),
            pltpu.VMEM((3, 256, 320), F32),
            pltpu.VMEM((256, 48), F32),
            pltpu.VMEM((48, 320), F32),
        ],
        compiler_params=pltpu.CompilerParams(vmem_limit_bytes=60 << 20 if width <= 2048 else 63 << 20),
    )(ds_ext, cot_ext, w1, wm, wl3, wlt, wmt, wf3)


def blur_step(n, with_target, *refs):
    refs = list(refs)
    take = lambda count: [refs.pop(0) for _ in range(count)]
    values_ref, tab_ref = take(2)
    extra_ref, = take(1)
    side_ref = take(1)[0] if with_target else None
    out_ref, other_ref = take(2)
    (send1, cols, padded, adj, send2, back, hx_send, hx_recv,
     s1, r1, s2, r2, hs, hr) = refs
    me = lax.axis_index("rows")
    width = values_ref.shape[1]
    height = BAND * n
    blocks = height // BLK

    def peer(k):
        return lax.rem(me + k, n)

    barrier = pltpu.get_barrier_semaphore()
    for k in range(1, n):
        pl.semaphore_signal(barrier, inc=1, device_id={"rows": peer(k)}, device_id_type=MESH)

    values = values_ref[...]
    wide = jnp.concatenate([values, jnp.zeros((BAND, BLK), F32)], axis=1)
    blurred = jnp.zeros((BAND, width), F32)
    for t in range(TAPS):
        moved = wide if t == RAD else pltpu.roll(wide, (RAD - t) % (width + BLK), 1)
        blurred = blurred + tab_ref[t : t + 1, 0:width] * moved[:, 0:width]
    for j in range(n):
        send1[j, 0:8, :] = blurred[:, j * BLK : j * BLK + BLK]
    if not with_target:
        for j in range(n):
            send1[j, 8:16, :] = extra_ref[j * 8 : j * 8 + 8, :]
    else:
        hx_send[0, 0:4, :] = values[4:8, :]
        hx_send[0, 4:8, :] = extra_ref[4:8, :]
        hx_send[1, 0:4, :] = values[0:4, :]
        hx_send[1, 4:8, :] = extra_ref[0:4, :]
    pl.semaphore_wait(barrier, n - 1)

    def exchange(src, dst, send_sem, recv_sem):
        copies = []
        for k in range(1, n):
            to = peer(k)
            copies.append(pltpu.make_async_remote_copy(
                src_ref=src.at[to], dst_ref=dst.at[me], send_sem=send_sem.at[k - 1], recv_sem=recv_sem.at[k - 1],
                device_id={"rows": to}, device_id_type=MESH))
        for copy in copies:
            copy.start()
        return copies

    first = exchange(send1, cols, s1, r1)
    near = []
    if with_target:
        for side, k in ((0, 1), (1, n - 1)):
            near.append(pltpu.make_async_remote_copy(
                src_ref=hx_send.at[side], dst_ref=hx_recv.at[side], send_sem=hs.at[side], recv_sem=hr.at[side],
                device_id={"rows": peer(k)}, device_id_type=MESH))
        for copy in near:
            copy.start()
    cols[me] = send1[me]
    for copy in first:
        copy.wait_recv()

    padded[...] = jnp.zeros_like(padded)
    for i in range(n):
        padded[16 + i * 8 : 24 + i * 8, :] = cols[i, 0:8, :]
    adj[...] = jnp.zeros_like(adj)
    results = []
    for blk in range(blocks):
        lanes = slice(width + BLK + blk * BLK, width + 2 * BLK + blk * BLK)
        total = jnp.zeros((BLK, BLK), F32)
        for t in range(TAPS):
            start = 16 + blk * BLK + t - RAD
            total = total + tab_ref[t : t + 1, lanes] * padded[start : start + BLK, :]
        if with_target:
            total = total - side_ref[blk * BLK : blk * BLK + BLK, :]
        results.append(total)
    padded[...] = jnp.zeros_like(padded)
    for blk in range(blocks):
        lanes = slice(width + BLK + blk * BLK, width + 2 * BLK + blk * BLK)
        padded[32 : 32 + BLK, :] = results[blk]
        total = jnp.zeros((BLK + 32, BLK), F32)
        for t in range(TAPS):
            start = 16 - t + RAD
            total = total + tab_ref[t : t + 1, lanes] * padded[start : start + BLK + 32, :]
        adj[blk * BLK : blk * BLK + BLK + 32, :] = adj[blk * BLK : blk * BLK + BLK + 32, :] + total
    adj[0:16, :] = jnp.zeros((16, BLK), F32)
    adj[16 + height : 32 + height, :] = jnp.zeros((16, BLK), F32)
    if with_target:
        sub = lax.broadcasted_iota(jnp.int32, (BAND, BLK), 0)
    else:
        share = cols[0, 8:16, :]
        for i in range(1, n):
            share = share + cols[i, 8:16, :]
    for i in range(n):
        base = 16 + i * 8
        send2[i, 0:8, :] = adj[base : base + 8, :]
        if with_target:
            send2[i, 8:16, :] = jnp.where(sub < 4, adj[base - 4 : base + 4, :], adj[base + 4 : base + 12, :])
        else:
            send2[i, 8:16, :] = share
    second = exchange(send2, back, s2, r2)
    back[me] = send2[me]
    for copy in second:
        copy.wait_recv()

    rows = 16 if with_target else 8
    pieces = [back[j, 0:rows, :] for j in range(n)] + [jnp.zeros((rows, BLK), F32)]
    wide = jnp.concatenate(pieces, axis=1)
    table_end = width + BLK
    total = jnp.zeros((rows, table_end), F32)
    for t in range(TAPS):
        part = tab_ref[t : t + 1, 0:table_end] * wide
        total = total + (part if t == RAD else pltpu.roll(part, (t - RAD) % table_end, 1))
    total = total[:, 0:width]
    if with_target:
        for copy in near:
            copy.wait_recv()
        out_ref[0:8, :] = values - STEP_SIZE * total[0:8, :]
        ends = jnp.concatenate([hx_recv[0, 0:4, :], hx_recv[1, 0:4, :]], axis=0)
        out_ref[8:16, :] = ends - STEP_SIZE * total[8:16, :]
        other_ref[0:8, :] = extra_ref[...]
        other_ref[8:16, :] = jnp.concatenate([hx_recv[0, 4:8, :], hx_recv[1, 4:8, :]], axis=0)
    else:
        out_ref[...] = values - STEP_SIZE * total
        for i in range(n):
            other_ref[i * 8 : i * 8 + 8, :] = back[i, 8:16, :]
    for copy in first + near + second:
        copy.wait_send()


def data_gradient(n, values, table, extra, observed):
    width = values.shape[1]
    with_target = observed is not None
    height = BAND * n
    deep = 16 if (with_target or extra is not None) else 8
    rows1 = 8 if with_target else deep
    args = (values, table, extra) + ((observed,) if with_target else ())
    if with_target:
        outs = (jax.ShapeDtypeStruct((16, width), F32), jax.ShapeDtypeStruct((16, width), F32))
    else:
        outs = (jax.ShapeDtypeStruct((8, width), F32), jax.ShapeDtypeStruct((8 * n, BLK), F32))
    return pl.pallas_call(
        functools.partial(blur_step, n, with_target),
        out_shape=outs,
        in_specs=[pl.BlockSpec(memory_space=pltpu.VMEM)] * len(args),
        out_specs=[pl.BlockSpec(memory_space=pltpu.VMEM)] * 2,
        scratch_shapes=[
            pltpu.VMEM((n, rows1, BLK), F32),
            pltpu.VMEM((n, rows1, BLK), F32),
            pltpu.VMEM((max(height, BLK) + 64, BLK), F32),
            pltpu.VMEM((height + 32, BLK), F32),
            pltpu.VMEM((n, deep, BLK), F32),
            pltpu.VMEM((n, deep, BLK), F32),
            pltpu.VMEM((2, 8, width if with_target else BLK), F32),
            pltpu.VMEM((2, 8, width if with_target else BLK), F32),
            pltpu.SemaphoreType.DMA((n - 1,)),
            pltpu.SemaphoreType.DMA((n - 1,)),
            pltpu.SemaphoreType.DMA((n - 1,)),
            pltpu.SemaphoreType.DMA((n - 1,)),
            pltpu.SemaphoreType.DMA((2,)),
            pltpu.SemaphoreType.DMA((2,)),
        ],
        compiler_params=pltpu.CompilerParams(
            collective_id=0 if with_target else 1, has_side_effects=True, vmem_limit_bytes=40 << 20),
    )(*args)


def tap_tables(zone_map, bank_pick, psf_bank, n, position, width, group_cols):
    norm_bank = psf_bank / jnp.sum(psf_bank, axis=1, keepdims=True)
    row_line = lax.dynamic_slice_in_dim(zone_map, position * BAND // BLK, 1, 0)[0]
    col_line = lax.dynamic_slice_in_dim(zone_map, position * group_cols // BLK, 1, 1)[:, 0]

    def pick(line, picks):
        zone = jnp.sum(jnp.where(line[:, None] == jnp.arange(picks.shape[0])[None, :], picks[None, :], 0), axis=1)
        hot = zone[None, :, None] == jnp.arange(psf_bank.shape[0])[None, None, :]
        return jnp.sum(jnp.where(hot, norm_bank.T[:, None, :], 0.0), axis=2)

    per_block = jnp.concatenate(
        [pick(row_line, bank_pick[0]), jnp.zeros((TAPS, 1), F32), pick(col_line, bank_pick[1])], axis=1)
    count = per_block.shape[1]
    return jnp.broadcast_to(per_block[:, :, None], (TAPS, count, BLK)).reshape(TAPS, count * BLK)


def on_device(n, estimate, observed, cotangent, zone_map, bank_pick, psf_bank, w_first, w_mid, w_last):
    width, group_cols = estimate.shape[1], observed.shape[1]
    position = lax.axis_index("rows")
    height = BAND * n
    scale = GRAD_FACTOR / math.sqrt(height * width)
    table = tap_tables(zone_map, bank_pick, psf_bank, n, position, width, group_cols)
    ds_ext, cot_ext = data_gradient(n, estimate, table, cotangent, observed)
    denoised, grad_data, shares = denoise(n, scale, ds_ext, cot_ext, w_first, w_mid, w_last)
    grad_estimate, sums = data_gradient(n, grad_data, table, shares, None)
    slots = sums[0:96].reshape(3, 32, 4, 32)
    grad_mid = jnp.transpose(slots, (1, 3, 0, 2)).reshape(32, 32, 12)[:, :, 0:9].reshape(32, 32, 3, 3)
    grad_first = sums[64:96, 32:41].reshape(32, 1, 3, 3)
    grad_last = jnp.transpose(sums[64:73, 64:96]).reshape(1, 32, 3, 3)
    return denoised, grad_estimate, grad_first, grad_mid, grad_last


def solution(mesh):
    placed = (
        P(("parts", "rows"), None),
        P("parts", "rows"),
        P(("parts", "rows"), None),
        P("parts", None),
        P(), P(), P(), P(), P(),
    )
    return jax.shard_map(
        functools.partial(on_device, mesh.shape["rows"]),
        mesh=mesh,
        in_specs=placed,
        out_specs=(
            P(("parts", "rows"), None),
            P(("parts", "rows"), None),
            P("parts", None, None, None),
            P("parts", None, None, None),
            P("parts", None, None, None),
        ),
        check_vma=False,
    )
```

time: 463 us -> 68.5 us (0.15); the launches traced: 456 us -> 68.1 us
  local copies, waits for them, and re-layouts: 139 us -> 13.4 us
  other arithmetic: 99.6 us -> 2.46 us
  matrix products: 80.2 us -> 0.92 us
  blocking collectives: 64.1 us -> 0 us
  starting transfers between devices: 55.3 us -> 0 us
  Pallas kernels: 0 us -> 50.5 us
  waiting for transfers between devices: 15.9 us -> 0 us
    conv_general_dilated x34 -> x0, local copies, waits for them, and re-layouts: 116 us -> none  [conv_rim(): lax.conv_general_dilated(padded[None], weight, (1, 1), padding, dimension...]
    psum x1 -> x0, blocking collectives: 64.1 us -> none  [on_device(): lax.psum((partial_grads[0] * grad_scale, partial_grads[1] * grad_scale, p...]
    mul x13 -> x0, other arithmetic: 63.2 us -> none  [the longest x10 62.5 us: blur_line(): spread = jnp.pad(factor * values, widths)]
    conv_general_dilated x6 -> x0, matrix products: 61 us -> none  [conv_rim(): lax.conv_general_dilated(padded[None], weight, (1, 1), padding, dimension...]
    pallas_call x0 -> x3, Pallas kernels: none -> 50.5 us  [the longest x2 29.8 us: data_gradient(): pl.pallas_call(functools.partial(blur_step, n, with_target), out_shape=ou...]
    ppermute x12 -> x0, starting transfers between devices: 29.6 us -> none  [the longest x6 21.6 us: padded_2(): before = lax.ppermute(last, axis, up)]
    all_to_all x4 -> x0, starting transfers between devices: 25.7 us -> none  [the longest x2 18.1 us: data_gradient(): lax.all_to_all(blurred, 'rows', split_axis=1, concat_axis=0, tiled=True)]
    convert_element_type x7 -> x0, other arithmetic: 20.3 us -> none  [the longest x2 10.5 us: denoise(): (conv_rim(cot_pad, flipped(w_last)) * silu_slope(pre_mid)).astype(jnp.bfl...]
  transfers between devices with their start and end apart: 16 -> 0, of which waited for: 6 -> 0; matrix products, arithmetic and copies ran while one was open for 16% -> 0% of each run, Pallas kernels for 0% -> 0%
where the time goes in v1:
time: 68.5 us; the launch traced here: 68.1 us
  Pallas kernels  50.5 us (74%)
  local copies, waits for them, and re-layouts  13.4 us (20%)
  other arithmetic  2.46 us (4%)
  matrix products  0.92 us (1%)
  between operations  0.92 us (1%)
    pallas_call x2, Pallas kernels, data_gradient(): pl.pallas_call(functools.partial(blur_step, n, with_target), out_shape=ou...  29.8 us
    pallas_call x1, Pallas kernels, denoise(): pl.pallas_call(functools.partial(denoise_kernel, n, scale), out_shape=(ja...  20.7 us
    unnamed x37, local copies, waits for them, and re-layouts  5.17 us
    reshape x6, local copies, waits for them, and re-layouts, ein(): jnp.einsum(spec, jnp.asarray(table, BF16), weight, preferred_element_type...  3.29 us

profile of v1, /device:TPU:0, one launch (start us, length us, event | category | flops | bytes accessed | tf_op | source)
XLA Modules:
  0.0 68.1 jit_solution(6108411183082388029)
XLA Ops:
  0.6 0.0 copy-start.16
  0.6 0.0 copy-start.8
  0.7 0.0 copy-start.15
  0.7 0.0 copy-start.7
  0.7 0.6 copy-done.16
  1.3 0.6 constant_dynamic-slice_fusion
  1.9 0.0 copy-done.8
  1.9 0.1 reduce_sum.48
  2.0 0.1 pad.1.clone
  2.1 0.0 copy-done.15
  2.1 1.3 %slice_bitcast_fusion.1 = (s32[8]{0:T(128)S(1)}, s32[]{:T(128)}) fusion(s32[2,8]{1,0:T(2,128)S(1)} %copy-done.15, s32[]{:T(128)} %bitcast.3), kind=kLoop, calls=%fused_computation.28 | loop fusion | flops 23 | bytes 104 | tf_op jit(solution)/shard_map/jit(_where)/broadcast_in_dim | solution.py:400
  3.3 0.1 select_reduce_fusion.2
  3.4 0.6 iota_compare_fusion.2
  4.1 0.1 iota_compare_fusion
  4.2 0.1 select_reduce_fusion.1
  4.3 0.1 select_reduce_fusion
  4.4 0.1 pad_maximum_fusion
  4.4 0.1 copy.50
  4.5 0.1 copy.58
  4.7 0.0 copy-start.12
  4.7 0.0 copy-start.14
  4.7 0.7 %reshape.101.wmt_ref = bf16[32,288]{1,0:T(8,128)(2,1)} reshape(bf16[32,3,3,32]{3,2,1,0:T(4,128)(2,1)S(1)} %copy.58) | data formatting | bytes 36864 | tf_op jit(solution)/shard_map/reshape | solution.py:197
  5.4 0.2 fusion.3
  5.7 0.0 copy-start.11
  5.7 0.0 copy-start.13
  5.7 0.7 %reshape.102.wf_ref = bf16[24,320]{1,0:T(8,128)(2,1)} reshape(bf16[3,8,10,32]{3,2,1,0:T(8,128)(2,1)S(1)} %copy.60) | data formatting | bytes 30720 | tf_op jit(solution)/shard_map/reshape | solution.py:190
  6.4 0.0 copy-done.11
  6.4 0.2 fusion.2
  6.7 0.7 %reshape.99.wl_ref = bf16[24,320]{1,0:T(8,128)(2,1)} reshape(bf16[3,8,10,32]{3,2,1,0:T(8,128)(2,1)S(1)} %copy.55) | data formatting | bytes 30720 | tf_op jit(solution)/shard_map/reshape | solution.py:190
  7.4 0.1 copy.53
  7.4 0.0 copy-start.10
  7.4 0.7 %reshape.98.wm_ref = bf16[32,288]{1,0:T(8,128)(2,1)} reshape(bf16[32,3,3,32]{3,2,1,0:T(4,128)(2,1)S(1)} %copy.53) | data formatting | bytes 36864 | tf_op jit(solution)/shard_map/reshape | solution.py:196
  8.2 0.2 fusion.1
  8.5 0.2 reshape.100
  8.6 0.0 copy-start.9
  8.6 0.8 %copy.62.wlt_ref = bf16[384,48]{1,0:T(8,128)(2,1)} copy(bf16[384,48]{0,1:T(8,128)(2,1)S(1)} %reshape.100) | data formatting | bytes 73728 | tf_op jit(solution)/shard_map/reshape | solution.py:190
  9.4 0.2 fusion
  9.6 0.1 copy.52
  9.7 0.2 reshape.97
  9.9 0.8 %copy.61.w1_ref = bf16[448,48]{1,0:T(8,128)(2,1)} copy(bf16[448,48]{0,1:T(8,128)(2,1)S(1)} %reshape.97) | data formatting | bytes 86016 | tf_op jit(solution)/shard_map/reshape | solution.py:190
  10.7 0.1 broadcast_in_dim.74
  10.8 0.0 copy-start.2
  10.8 0.0 copy-start.3
  10.9 0.0 copy-start.4
  10.9 0.1 copy.71
  10.9 0.7 %copy-done.2 = f32[8,2048]{1,0:T(8,128)S(1)} copy-done((f32[8,2048]{1,0:T(8,128)S(1)}, f32[8,2048]{1,0:T(8,128)}, u32[]{:S(2)}) %copy-start.2) | copy-done | bytes 65560
  11.7 0.0 copy-done.3
  11.7 0.0 copy-done.4
  11.7 16.4 %shard_map.164 = (f32[16,2048]{1,0:T(8,128)S(1)}, f32[16,2048]{1,0:T(8,128)S(1)}) custom-call(f32[8,2048]{1,0:T(8,128)S(1)} %copy-done.2, f32[25,2304]{1,0:T(8,128)S(1)} %bitcast.67, f32[8,2048]{1,0:T(8,128)S(1)} %copy-done.3, f32[128,128]{1,0:T(8,128)S(1)} %copy-done.4), custom_call_target="tpu_custom_call" | custom-call | tf_op jit(solution)/shard_map/pallas_call | solution.py:368
  28.1 0.0 copy-start
  28.1 0.6 copy-done
  28.8 0.7 copy-done.1
  29.4 20.7 %shard_map.165 = (f32[8,2048]{1,0:T(8,128)}, f32[8,2048]{1,0:T(8,128)}, f32[128,128]{1,0:T(8,128)}) custom-call(f32[16,2048]{1,0:T(8,128)} %copy-done, f32[16,2048]{1,0:T(8,128)} %copy-done.1, bf16[448,48]{1,0:T(8,128)(2,1)} %copy.61.w1_ref, bf16[32,288]{1,0:T(8,128)(2,1)} %reshape.98.wm_ref, bf16[24,320]{1,0:T(8,128)(2,1)} %reshape.99.wl_ref, ...), custom_call_target="tpu_custom_call" | custom-call | tf_op jit(solution)/shard_map/pallas_call | solution.py:198
  50.1 0.8 %copy-done.5 = f32[8,2048]{1,0:T(8,128)S(1)} copy-done((f32[8,2048]{1,0:T(8,128)S(1)}, f32[8,2048]{1,0:T(8,128)}, u32[]{:S(2)}) %copy-start.5) | copy-done | bytes 65560
  50.9 0.8 %copy-done.6 = f32[128,128]{1,0:T(8,128)S(1)} copy-done((f32[128,128]{1,0:T(8,128)S(1)}, f32[128,128]{1,0:T(8,128)}, u32[]{:S(2)}) %copy-start.6) | copy-done | bytes 65560
  51.8 13.4 %shard_map.166 = (f32[8,2048]{1,0:T(8,128)S(1)}, f32[128,128]{1,0:T(8,128)S(1)}) custom-call(f32[8,2048]{1,0:T(8,128)S(1)} %copy-done.5, f32[25,2304]{1,0:T(8,128)S(1)} %bitcast.68, f32[128,128]{1,0:T(8,128)S(1)} %copy-done.6), custom_call_target="tpu_custom_call" | custom-call | tf_op jit(solution)/shard_map/pallas_call | solution.py:368
  65.2 0.1 slice_bitcast_fusion
  65.3 0.6 reshape.117
  65.9 0.1 slice.20
  66.0 0.1 copy.63
  66.0 0.6 reshape.116
  66.7 0.1 reshape.104
  66.8 0.7 slice.24
  67.5 0.6 copy.89
  (16 shorter events, 0.1 us)
Async XLA Ops:
  0.6 0.7 copy-start.16
  0.6 1.2 %copy-start.8 = (f32[8,25]{1,0:T(8,128)S(1)}, f32[8,25]{1,0:T(8,128)}, u32[]{:S(2)}) copy-start(f32[8,25]{1,0:T(8,128)} %param.18) | copy-start | bytes 2404
  0.7 1.4 %copy-start.15 = (s32[2,8]{1,0:T(2,128)S(1)}, s32[2,8]{1,0:T(2,128)}, u32[]{:S(2)}) copy-start(s32[2,8]{1,0:T(2,128)} %param.17) | copy-start | bytes 196
  0.7 3.9 %copy-start.7 = (bf16[32,32,3,3]{1,0,3,2:T(8,128)(2,1)S(1)}, bf16[32,32,3,3]{1,0,3,2:T(8,128)(2,1)}, u32[]{:S(2)}) copy-start(bf16[32,32,3,3]{1,0,3,2:T(8,128)(2,1)} %param.20) | copy-start | bytes 55300
  4.7 0.8 %copy-start.12 = (bf16[32,1,3,3]{0,3,2,1:T(4,128)(2,1)S(1)}, bf16[32,1,3,3]{0,3,2,1:T(4,128)(2,1)}, u32[]{:S(2)}) copy-start(bf16[32,1,3,3]{0,3,2,1:T(4,128)(2,1)} %param.19) | copy-start | bytes 1732
  4.7 0.7 %copy-start.14 = (bf16[8,10,3,1]{1,2,3,0:T(4,128)(2,1)S(1)}, bf16[8,10,3,1]{1,2,3,0:T(4,128)(2,1)}, u32[]{:S(2)}) copy-start(bf16[8,10,3,1]{1,2,3,0:T(4,128)(2,1)} %constant.53) | copy-start | bytes 1444
  5.7 0.7 %copy-start.11 = (bf16[1,32,3,3]{1,3,2,0:T(4,128)(2,1)S(1)}, bf16[1,32,3,3]{1,3,2,0:T(4,128)(2,1)}, u32[]{:S(2)}) copy-start(bf16[1,32,3,3]{1,3,2,0:T(4,128)(2,1)} %param.21) | copy-start | bytes 1732
  5.7 0.7 %copy-start.13 = (bf16[8,10,3,1]{1,2,3,0:T(4,128)(2,1)S(1)}, bf16[8,10,3,1]{1,2,3,0:T(4,128)(2,1)}, u32[]{:S(2)}) copy-start(bf16[8,10,3,1]{1,2,3,0:T(4,128)(2,1)} %constant.51) | copy-start | bytes 1444
  7.4 0.7 %copy-start.10 = (bf16[12,16,3,1]{1,2,3,0:T(4,128)(2,1)S(1)}, bf16[12,16,3,1]{1,2,3,0:T(4,128)(2,1)}, u32[]{:S(2)}) copy-start(bf16[12,16,3,1]{1,2,3,0:T(4,128)(2,1)} %constant.52) | copy-start | bytes 3460
  8.6 0.8 %copy-start.9 = (bf16[14,16,3,1]{1,2,3,0:T(4,128)(2,1)S(1)}, bf16[14,16,3,1]{1,2,3,0:T(4,128)(2,1)}, u32[]{:S(2)}) copy-start(bf16[14,16,3,1]{1,2,3,0:T(4,128)(2,1)} %constant.50) | copy-start | bytes 4036
  10.8 0.8 %copy-start.2 = (f32[8,2048]{1,0:T(8,128)S(1)}, f32[8,2048]{1,0:T(8,128)}, u32[]{:S(2)}) copy-start(f32[8,2048]{1,0:T(8,128)} %refs_0_.1) | copy-start | bytes 196612
  10.8 0.9 %copy-start.3 = (f32[8,2048]{1,0:T(8,128)S(1)}, f32[8,2048]{1,0:T(8,128)}, u32[]{:S(2)}) copy-start(f32[8,2048]{1,0:T(8,128)} %refs_2_.1) | copy-start | bytes 196612
  10.9 0.9 %copy-start.4 = (f32[128,128]{1,0:T(8,128)S(1)}, f32[128,128]{1,0:T(8,128)}, u32[]{:S(2)}) copy-start(f32[128,128]{1,0:T(8,128)} %refs_3_.1) | copy-start | bytes 196612
  28.1 0.7 copy-start
  28.8 0.7 copy-start.1
  50.1 0.8 %copy-start.5 = (f32[8,2048]{1,0:T(8,128)S(1)}, f32[8,2048]{1,0:T(8,128)}, u32[]{:S(2)}) copy-start(f32[8,2048]{1,0:T(8,128)} %get-tuple-element.15.refs_0_) | copy-start | bytes 196612
  50.9 0.8 %copy-start.6 = (f32[128,128]{1,0:T(8,128)S(1)}, f32[128,128]{1,0:T(8,128)}, u32[]{:S(2)}) copy-start(f32[128,128]{1,0:T(8,128)} %get-tuple-element.16.refs_2_) | copy-start | bytes 196612

commit v2 on v1

v2 whole, which is shorter than its diff:
```python
import functools
import math

import jax
import jax.numpy as jnp
from jax import lax
from jax.experimental import pallas as pl
from jax.experimental.pallas import tpu as pltpu
from jax.sharding import PartitionSpec as P

BLK = 128
RAD = 12
TAPS = 2 * RAD + 1
CH = 32
BAND = 8
STEP_SIZE = 2.0
GRAD_FACTOR = 8.0
MESH = pl.DeviceIdType.MESH
F32 = jnp.float32
BF16 = jnp.bfloat16

EXT_ROWS = list(range(8)) + [-4, -3, -2, -1, 8, 9, 10, 11]


ROWS_14 = list(range(-3, 11))
ROWS_12 = list(range(-2, 10))
ROWS_10 = list(range(-1, 9))
ROWS_8 = list(range(8))


def silu_pair(v):
    s = 0.5 * jnp.tanh(0.5 * v) + 0.5
    return v * s, s * (1.0 + v * (1.0 - s))


def shifted(v, delta):
    width = v.shape[1]
    lane = lax.broadcasted_iota(jnp.int32, v.shape, 1)
    if delta == 1:
        return jnp.where(lane < width - 1, pltpu.roll(v, width - 1, 1), 0.0)
    return jnp.where(lane > 0, pltpu.roll(v, 1, 1), 0.0)


def nt_dot(a, b):
    return lax.dot_general(a, b, (((1,), (1,)), ((), ())), preferred_element_type=F32)


def iota(shape, dim):
    return lax.broadcasted_iota(jnp.int32, shape, dim)


def third(v, size):
    return (v >= size).astype(jnp.int32) + (v >= 2 * size).astype(jnp.int32)


def ones_where(cond):
    return jnp.where(cond, 1.0, 0.0).astype(BF16)


def build_table(n, tab, zone_ref, pick_ref, psf_ref, hot, blocks_row, blocks_col):
    me = lax.axis_index("rows")
    row = iota((8, BLK), 0)
    for i in range(blocks_row):
        k = pick_ref[0, zone_ref[me * BAND // BLK, i]]
        hot[:, i * BLK : i * BLK + BLK] = jnp.where(row == k, 1.0, 0.0)
    hot[:, blocks_row * BLK : blocks_row * BLK + BLK] = jnp.zeros((8, BLK), F32)
    for i in range(blocks_col):
        k = pick_ref[1, zone_ref[i, me]]
        at = (blocks_row + 1 + i) * BLK
        hot[:, at : at + BLK] = jnp.where(row == k, 1.0, 0.0)
    psf = psf_ref[...]
    norm = psf / jnp.sum(psf, axis=1, keepdims=True)
    tab[0:TAPS, :] = lax.dot_general(
        norm, hot[...], (((0,), (0,)), ((), ())), preferred_element_type=F32, precision=lax.Precision.HIGHEST)


def build_weights(wf_ref, wl_ref, w2_ref, wsel, w1, wlt, wl3, wf3, wmb, wmtb):
    k, lane = iota((9, 48), 0), iota((9, 48), 1)
    ka = third(k, 3)
    kb = k - 3 * ka
    lb = third(lane, 16)
    le = lane - 16 * lb
    same = kb == lb

    def select(row, sign):
        hit = None
        for a in range(3):
            q = row + sign * (a - 1)
            if q in EXT_ROWS:
                here = jnp.logical_and(ka == a, le == EXT_ROWS.index(q))
                hit = here if hit is None else jnp.logical_or(hit, here)
        return ones_where(jnp.logical_and(same, hit))

    for i, r in enumerate(ROWS_14):
        w1[i * 32 : i * 32 + 32, :] = jnp.dot(wf_ref[...], select(r, 1), preferred_element_type=F32).astype(BF16)
    for i, r in enumerate(ROWS_12):
        wlt[i * 32 : i * 32 + 32, :] = jnp.dot(wl_ref[...], select(r, -1), preferred_element_type=F32).astype(BF16)
    out, k = iota((24, 9), 0), iota((24, 9), 1)
    ob = third(out, 8)
    orow = out - 8 * ob
    ka = third(k, 3)
    same = k - 3 * ka == ob
    for i, q in enumerate(ROWS_10):
        fwd = ones_where(jnp.logical_and(same, ka == q - orow + 1))
        wl3[:, i * 32 : i * 32 + 32] = nt_dot(fwd, wl_ref[...]).astype(BF16)
        adj = ones_where(jnp.logical_and(same, ka == orow - q + 1))
        wf3[:, i * 32 : i * 32 + 32] = nt_dot(adj, wf_ref[...]).astype(BF16)
    k, m = iota((288, 288), 0), iota((288, 288), 1)
    mb = third(m, 96)
    rest = m - 96 * mb
    ma = third(rest, 32)
    order = ones_where(k == (rest - 32 * ma) * 9 + ma * 3 + mb)
    wm = jnp.dot(w2_ref[...], order, preferred_element_type=F32).astype(BF16)
    wsel[...] = wm
    eye = ones_where(iota((32, 32), 0) == iota((32, 32), 1))
    wmb[...] = jnp.zeros_like(wmb)
    wmtb[...] = jnp.zeros_like(wmtb)
    for b in range(3):
        for r in range(12):
            wmb[r * 32 : r * 32 + 32, b * 448 + r * 32 : b * 448 + r * 32 + 96] = wsel[:, b * 96 : b * 96 + 96]
        turned = [nt_dot(eye, wsel[:, b * 96 + (2 - a) * 32 : b * 96 + (2 - a) * 32 + 32]) for a in range(3)]
        turned = jnp.concatenate(turned, axis=1).astype(BF16)
        for r in range(10):
            wmtb[r * 32 : r * 32 + 32, b * 384 + r * 32 : b * 384 + r * 32 + 96] = turned


def row_blur(values, tab):
    width = values.shape[1]
    wide = jnp.concatenate([values, jnp.zeros((BAND, BLK), F32)], axis=1)
    blurred = jnp.zeros((BAND, width), F32)
    for t in range(TAPS):
        moved = wide if t == RAD else pltpu.roll(wide, (RAD - t) % (width + BLK), 1)
        blurred = blurred + tab[t : t + 1, 0:width] * moved[:, 0:width]
    return blurred


def row_blur_adjoint(back, rows, n, width, tab):
    end = width + BLK
    wide = jnp.concatenate([back[j] for j in range(n)] + [jnp.zeros((rows, BLK), F32)], axis=1)
    total = jnp.zeros((rows, end), F32)
    for t in range(TAPS):
        part = tab[t : t + 1, 0:end] * wide
        total = total + (part if t == RAD else pltpu.roll(part, (t - RAD) % end, 1))
    return total[:, 0:width]


def column_pass(n, width, cols, padded, adj, tab, target):
    height = BAND * n
    blocks = height // BLK
    padded[...] = jnp.zeros_like(padded)
    for i in range(n):
        padded[16 + i * 8 : 24 + i * 8, :] = cols[i]
    results = []
    for blk in range(blocks):
        lanes = slice(width + (blk + 1) * BLK, width + (blk + 2) * BLK)
        total = jnp.zeros((BLK, BLK), F32)
        for t in range(TAPS):
            start = 16 + blk * BLK + t - RAD
            total = total + tab[t : t + 1, lanes] * padded[start : start + BLK, :]
        if target is not None:
            total = total - target[blk * BLK : blk * BLK + BLK, :]
        results.append(total)
    padded[...] = jnp.zeros_like(padded)
    adj[...] = jnp.zeros_like(adj)
    for blk in range(blocks):
        lanes = slice(width + (blk + 1) * BLK, width + (blk + 2) * BLK)
        padded[32 : 32 + BLK, :] = results[blk]
        total = jnp.zeros((BLK + 32, BLK), F32)
        for t in range(TAPS):
            start = 16 - t + RAD
            total = total + tab[t : t + 1, lanes] * padded[start : start + BLK + 32, :]
        adj[blk * BLK : blk * BLK + BLK + 32, :] = adj[blk * BLK : blk * BLK + BLK + 32, :] + total
    adj[0:16, :] = jnp.zeros((16, BLK), F32)
    adj[16 + height : 32 + height, :] = jnp.zeros((16, BLK), F32)


def kernel(
    n, scale,
    est_ref, obs_ref, cot_in_ref, zone_ref, pick_ref, psf_ref, wf_ref, wl_ref, w2_ref,
    den_ref, ge_ref, sums_ref,
    tab, hot, send1, cols1, send2, back2, send3, cols3, send4, back4, share, share_in, whole, padded, adj,
    hx_send, hx_recv, ds_ref, cot_ref,
    wsel, w1, wlt, wl3, wf3, wmb, wmtb, f3, c3, pre1, x3, pm, mid, bfr, d24, gm_acc, gf_acc, gl_acc,
    send_sems, recv_sems, hs, hr,
):
    me = lax.axis_index("rows")
    width = est_ref.shape[1]
    step = bfr.shape[1]
    chunks = width // step
    first, last = me == 0, me == n - 1
    started = []

    def peer(k):
        return lax.rem(me + k, n)

    barrier = pltpu.get_barrier_semaphore()
    for k in range(1, n):
        pl.semaphore_signal(barrier, inc=1, device_id={"rows": peer(k)}, device_id_type=MESH)

    def exchange(index, src_at, dst):
        copies = []
        for k in range(1, n):
            to = peer(k)
            copies.append(pltpu.make_async_remote_copy(
                src_ref=src_at(to), dst_ref=dst.at[me],
                send_sem=send_sems.at[index, k - 1], recv_sem=recv_sems.at[index, k - 1],
                device_id={"rows": to}, device_id_type=MESH))
        for copy in copies:
            copy.start()
        started.extend(copies)
        return copies

    def arrive(copies):
        for copy in copies:
            copy.wait_recv()

    build_table(n, tab, zone_ref, pick_ref, psf_ref, hot, width // BLK, BAND * n // BLK)
    blurred = row_blur(est_ref[...], tab)
    for j in range(n):
        send1[j] = blurred[:, j * BLK : j * BLK + BLK]
    hx_send[0, 0:4, :] = est_ref[4:8, :]
    hx_send[0, 4:8, :] = cot_in_ref[4:8, :]
    hx_send[1, 0:4, :] = est_ref[0:4, :]
    hx_send[1, 4:8, :] = cot_in_ref[0:4, :]
    pl.semaphore_wait(barrier, n - 1)
    copies1 = exchange(0, lambda to: send1.at[to], cols1)
    near = []
    for side, k in ((0, 1), (1, n - 1)):
        near.append(pltpu.make_async_remote_copy(
            src_ref=hx_send.at[side], dst_ref=hx_recv.at[side], send_sem=hs.at[side], recv_sem=hr.at[side],
            device_id={"rows": peer(k)}, device_id_type=MESH))
    for copy in near:
        copy.start()
    cols1[me] = send1[me]
    build_weights(wf_ref, wl_ref, w2_ref, wsel, w1, wlt, wl3, wf3, wmb, wmtb)
    arrive(copies1)
    column_pass(n, width, cols1, padded, adj, tab, obs_ref)
    sub = iota((BAND, BLK), 0)
    for i in range(n):
        base = 16 + i * 8
        send2[i, 0:8, :] = adj[base : base + 8, :]
        send2[i, 8:16, :] = jnp.where(sub < 4, adj[base - 4 : base + 4, :], adj[base + 4 : base + 12, :])
    copies2 = exchange(1, lambda to: send2.at[to], back2)
    back2[me] = send2[me]

    sub = iota((16, width), 0)
    outside = jnp.logical_or(
        jnp.logical_and(jnp.logical_and(sub >= 8, sub < 12), first), jnp.logical_and(sub >= 12, last))
    arrive(near)
    cot_ref[0:8, :] = cot_in_ref[...]
    cot_ref[8:12, :] = hx_recv[0, 4:8, :]
    cot_ref[12:16, :] = hx_recv[1, 4:8, :]
    ds_ref[0:8, :] = est_ref[...]
    ds_ref[8:12, :] = hx_recv[0, 0:4, :]
    ds_ref[12:16, :] = hx_recv[1, 0:4, :]
    cot = jnp.where(outside, 0.0, cot_ref[...])
    c3[0:16, :] = shifted(cot, 1).astype(BF16)
    c3[16:32, :] = cot.astype(BF16)
    c3[32:48, :] = shifted(cot, -1).astype(BF16)
    arrive(copies2)

    ds = ds_ref[...] - STEP_SIZE * row_blur_adjoint(back2, 16, n, width, tab)
    ds = jnp.where(outside, 0.0, ds)
    ds_ref[...] = ds
    f3[0:16, :] = shifted(ds, -1).astype(BF16)
    f3[16:32, :] = ds.astype(BF16)
    f3[32:48, :] = shifted(ds, 1).astype(BF16)

    def valid(row):
        below = jnp.logical_and(row < 0, first)
        above = jnp.logical_and(row >= BAND, last)
        return jnp.logical_not(jnp.logical_or(below, above))

    def at(i):
        return pl.ds(pl.multiple_of(i * step, step), step)

    def grp(i):
        return pl.ds(pl.multiple_of(i * 32, 32), 32)

    @pl.loop(0, chunks)
    def _(i):
        pre1[:, at(i)] = jnp.dot(w1[...], f3[:, at(i)], preferred_element_type=F32).astype(pre1.dtype)

    @pl.loop(0, 14)
    def _(r):
        act, slope = silu_pair(pre1[grp(r), :].astype(F32))
        act = jnp.where(valid(r - 3), act, 0.0)
        pre1[grp(r), :] = slope.astype(pre1.dtype)
        x3[grp(r), :] = shifted(act, -1).astype(BF16)
        x3[grp(r + 14), :] = act.astype(BF16)
        x3[grp(r + 28), :] = shifted(act, 1).astype(BF16)

    @pl.loop(0, chunks)
    def _(i):
        pm[:, at(i)] = jnp.dot(wmb[...], x3[:, at(i)], preferred_element_type=F32).astype(pm.dtype)

    @pl.loop(0, 12)
    def _(r):
        act, slope = silu_pair(pm[grp(r), :].astype(F32))
        act = jnp.where(valid(r - 2), act, 0.0)
        slope = jnp.where(valid(r - 2), slope, 0.0)
        pm[grp(r), :] = slope.astype(pm.dtype)
        mid[grp(r), :] = act.astype(BF16)

    gl_acc[...] = jnp.zeros_like(gl_acc)

    @pl.loop(0, chunks)
    def _(i):
        part = mid[32:352, at(i)]
        d24[:, at(i)] = jnp.dot(wl3[...], part, preferred_element_type=F32)
        gl_acc[...] += nt_dot(c3[:, at(i)], part)
        back = pm[:, at(i)].astype(F32) * jnp.dot(wlt[...], c3[:, at(i)], preferred_element_type=F32)
        pm[:, at(i)] = back.astype(pm.dtype)

    den_ref[...] = ds_ref[0:8, :] + d24[8:16, :] + shifted(d24[0:8, :], -1) + shifted(d24[16:24, :], 1)

    @pl.loop(0, 12)
    def _(r):
        back = pm[grp(r), :].astype(F32)
        x3[grp(r), :] = shifted(back, 1).astype(BF16)
        mid[grp(r), :] = back.astype(BF16)
        x3[grp(r + 28), :] = shifted(back, -1).astype(BF16)

    gf_acc[...] = jnp.zeros_like(gf_acc)
    row = iota((320, step), 0)
    gone = jnp.logical_or(jnp.logical_and(row < 32, first), jnp.logical_and(row >= 288, last))

    @pl.loop(0, chunks)
    def _(i):
        back = (
            jnp.dot(wmtb[:, 0:384], x3[0:384, at(i)], preferred_element_type=F32)
            + jnp.dot(wmtb[:, 384:768], mid[:, at(i)], preferred_element_type=F32)
            + jnp.dot(wmtb[:, 768:1152], x3[896:1280, at(i)], preferred_element_type=F32)
        ) * pre1[64:384, at(i)].astype(F32)
        back = jnp.where(gone, 0.0, back).astype(BF16)
        bfr[...] = back
        d24[:, at(i)] = jnp.dot(wf3[...], back, preferred_element_type=F32)
        gf_acc[...] += nt_dot(bfr[32:288, :], f3[:, at(i)])

    ge_ref[...] = cot_ref[0:8, :] + d24[8:16, :] + shifted(d24[0:8, :], 1) + shifted(d24[16:24, :], -1)
    blurred = row_blur(ge_ref[...], tab)
    for j in range(n):
        send3[j] = blurred[:, j * BLK : j * BLK + BLK]
    copies3 = exchange(2, lambda to: send3.at[to], cols3)
    cols3[me] = send3[me]

    gm_acc[...] = jnp.zeros_like(gm_acc)

    @pl.loop(0, chunks)
    def _(i):
        act = x3[448 + 64 : 448 + 384, at(i)]
        gm_acc[0] += nt_dot(x3[64:320, at(i)], act)
        gm_acc[1] += nt_dot(mid[64:320, at(i)], act)
        gm_acc[2] += nt_dot(x3[896 + 64 : 896 + 320, at(i)], act)

    share[...] = jnp.zeros_like(share)
    for a in range(3):
        for b in range(3):
            total = gm_acc[b, 0:32, a * 32 : a * 32 + 32]
            for r in range(1, 8):
                total = total + gm_acc[b, r * 32 : r * 32 + 32, (r + a) * 32 : (r + a) * 32 + 32]
            slot = a * 3 + b
            share[slot // 4 * 32 : slot // 4 * 32 + 32, slot % 4 * 32 : slot % 4 * 32 + 32] = total * scale
            total_first = jnp.zeros((32, 1), F32)
            total_last = jnp.zeros((1, 32), F32)
            for r in range(8):
                col = b * 16 + EXT_ROWS.index(r + a - 1)
                total_first = total_first + gf_acc[r * 32 : r * 32 + 32, col : col + 1]
                total_last = total_last + gl_acc[b * 16 + r : b * 16 + r + 1, (r + a) * 32 : (r + a) * 32 + 32]
            share[64:96, 32 + slot : 33 + slot] = total_first * scale
            share[64 + slot : 65 + slot, 64:96] = total_last * scale

    def eight(i):
        return pl.ds(pl.multiple_of(i * 8, 8), 8)

    copies5 = exchange(4, lambda to: share.at[eight(to)], share_in)
    share_in[me] = share[eight(me), :]
    arrive(copies3)
    column_pass(n, width, cols3, padded, adj, tab, None)
    for i in range(n):
        send4[i] = adj[16 + i * 8 : 24 + i * 8, :]
    copies4 = exchange(3, lambda to: send4.at[to], back4)
    back4[me] = send4[me]
    arrive(copies5)
    total = share_in[0]
    for i in range(1, n):
        total = total + share_in[i]
    whole[me] = total
    copies6 = exchange(5, lambda to: whole.at[me], whole)
    arrive(copies4)
    ge_ref[...] = ge_ref[...] - STEP_SIZE * row_blur_adjoint(back4, 8, n, width, tab)
    arrive(copies6)
    for i in range(n):
        sums_ref[i * 8 : i * 8 + 8, :] = whole[i]
    for copy in started + near:
        copy.wait_send()


def on_device(n, estimate, observed, cotangent, zone_map, bank_pick, psf_bank, w_first, w_mid, w_last):
    width = estimate.shape[1]
    height = BAND * n
    scale = GRAD_FACTOR / math.sqrt(height * width)
    keep = F32 if width <= 4096 else BF16
    step = 512 if width % 512 == 0 else BLK
    table = width + BLK + height
    vmem, smem = pl.BlockSpec(memory_space=pltpu.VMEM), pl.BlockSpec(memory_space=pltpu.SMEM)
    block = pltpu.VMEM((n, 8, BLK), F32)
    tall = pltpu.VMEM((n, 16, BLK), F32)
    denoised, grad_estimate, sums = pl.pallas_call(
        functools.partial(kernel, n, scale),
        out_shape=(
            jax.ShapeDtypeStruct((8, width), F32),
            jax.ShapeDtypeStruct((8, width), F32),
            jax.ShapeDtypeStruct((8 * n, BLK), F32),
        ),
        in_specs=[vmem, vmem, vmem, smem, smem, vmem, vmem, vmem, vmem],
        out_specs=[vmem] * 3,
        scratch_shapes=[
            pltpu.VMEM((32, table), F32),
            pltpu.VMEM((8, table), F32),
            block, block, tall, tall, block, block, block, block,
            pltpu.VMEM((8 * n, BLK), F32), block, block,
            pltpu.VMEM((max(height, BLK) + 64, BLK), F32),
            pltpu.VMEM((height + 32, BLK), F32),
            pltpu.VMEM((2, 8, width), F32),
            pltpu.VMEM((2, 8, width), F32),
            pltpu.VMEM((16, width), F32),
            pltpu.VMEM((16, width), F32),
            pltpu.VMEM((32, 288), BF16),
            pltpu.VMEM((448, 48), BF16),
            pltpu.VMEM((384, 48), BF16),
            pltpu.VMEM((24, 320), BF16),
            pltpu.VMEM((24, 320), BF16),
            pltpu.VMEM((384, 1344), BF16),
            pltpu.VMEM((320, 1152), BF16),
            pltpu.VMEM((48, width), BF16),
            pltpu.VMEM((48, width), BF16),
            pltpu.VMEM((448, width), keep),
            pltpu.VMEM((1344, width), BF16),
            pltpu.VMEM((384, width), keep),
            pltpu.VMEM((384, width), BF16),
            pltpu.VMEM((320, step), BF16),
            pltpu.VMEM((24, width), F32),
            pltpu.VMEM((3, 256, 320), F32),
            pltpu.VMEM((256, 48), F32),
            pltpu.VMEM((48, 320), F32),
            pltpu.SemaphoreType.DMA((6, n - 1)),
            pltpu.SemaphoreType.DMA((6, n - 1)),
            pltpu.SemaphoreType.DMA((2,)),
            pltpu.SemaphoreType.DMA((2,)),
        ],
        compiler_params=pltpu.CompilerParams(
            collective_id=0, has_side_effects=True, vmem_limit_bytes=56 << 20 if width <= 4096 else 64 << 20),
    )(estimate, observed, cotangent, zone_map, bank_pick, psf_bank,
      w_first.reshape(32, 9), w_last.reshape(32, 9), w_mid.reshape(32, 288))
    slots = sums[0:96].reshape(3, 32, 4, 32)
    grad_mid = jnp.transpose(slots, (1, 3, 0, 2)).reshape(32, 32, 12)[:, :, 0:9].reshape(32, 32, 3, 3)
    grad_first = sums[64:96, 32:41].reshape(32, 1, 3, 3)
    grad_last = jnp.transpose(sums[64:73, 64:96]).reshape(1, 32, 3, 3)
    return denoised, grad_estimate, grad_first, grad_mid, grad_last


def solution(mesh):
    placed = (
        P(("parts", "rows"), None),
        P("parts", "rows"),
        P(("parts", "rows"), None),
        P("parts", None),
        P(), P(), P(), P(), P(),
    )
    return jax.shard_map(
        functools.partial(on_device, mesh.shape["rows"]),
        mesh=mesh,
        in_specs=placed,
        out_specs=(
            P(("parts", "rows"), None),
            P(("parts", "rows"), None),
            P("parts", None, None, None),
            P("parts", None, None, None),
            P("parts", None, None, None),
        ),
        check_vma=False,
    )
```

time: 68.5 us -> 58.8 us (0.86)
  local copies, waits for them, and re-layouts: 13.4 us -> 9.26 us
  other arithmetic: 2.46 us -> 0 us
  Pallas kernels: 50.5 us -> 48.4 us
  matrix products: 0.92 us -> 0 us
    unnamed x37 -> x11, local copies, waits for them, and re-layouts: 5.17 us -> 2.65 us
    pallas_call x3 -> x1, Pallas kernels: 50.5 us -> 48.4 us  [on_device(): pl.pallas_call(functools.partial(kernel, n, scale), out_shape=(jax.ShapeD...]
    reshape x8 -> x6, local copies, waits for them, and re-layouts: 4.75 us -> 2.86 us  [the longest x2 1.39 us: on_device(): w_first.reshape(32, 9)]
    broadcast_in_dim x1 -> x0, other arithmetic: 1.28 us -> none  [pick(): jnp.where(line[:, None] == jnp.arange(picks.shape[0])[None, :], picks[Non...]
    dot_general x4 -> x0, matrix products: 0.92 us -> none  [ein(): jnp.einsum(spec, jnp.asarray(table, BF16), weight, preferred_element_type...]
    transpose x1, local copies, waits for them, and re-layouts: 0.07 us -> 0.83 us  [on_device(): grad_last = jnp.transpose(sums[64:73, 64:96]).reshape(1, 32, 3, 3)]
    eq x2 -> x0, other arithmetic: 0.72 us -> none  [pick(): hot = zone[None, :, None] == jnp.arange(psf_bank.shape[0])[None, None, :]]
    slice x2, local copies, waits for them, and re-layouts: 0.15 us -> 0.87 us  [on_device(): grad_first = sums[64:96, 32:41].reshape(32, 1, 3, 3)]
where the time goes in v2:
time: 58.8 us; the launch traced here: 58.3 us
  Pallas kernels  48.4 us (82%)
  local copies, waits for them, and re-layouts  9.26 us (16%)
  between operations  0.7 us (1%)
    pallas_call x1, Pallas kernels, on_device(): pl.pallas_call(functools.partial(kernel, n, scale), out_shape=(jax.ShapeD...  48.4 us
    unnamed x11, local copies, waits for them, and re-layouts  2.65 us
    reshape x2, local copies, waits for them, and re-layouts, on_device(): w_first.reshape(32, 9)  1.39 us

profile of v2, /device:TPU:0, one launch (start us, length us, event | category | flops | bytes accessed | tf_op | source)
XLA Modules:
  0.0 58.3 jit_solution(13856761102856940351)
XLA Ops:
  0.6 0.7 %reshape.34 = bf16[32,9]{0,1:T(8,128)(2,1)S(1)} reshape(bf16[32,1,3,3]{0,3,2,1:T(4,128)(2,1)} %param.15) | data formatting | bytes 1152 | tf_op jit(solution)/shard_map/reshape | solution.py:455
  1.3 0.0 copy-start.3
  1.3 0.7 %copy.20.wf_ref = bf16[32,9]{1,0:T(8,128)(2,1)} copy(bf16[32,9]{0,1:T(8,128)(2,1)S(1)} %reshape.34) | data formatting | bytes 1152 | tf_op jit(solution)/shard_map/reshape | solution.py:455
  2.0 0.0 copy-done.3
  2.0 0.7 %copy.21.wl_ref = bf16[32,9]{1,0:T(8,128)(2,1)} copy(bf16[32,9]{0,1:T(8,128)(2,1)S(1)} %reshape.35) | data formatting | bytes 1152 | tf_op jit(solution)/shard_map/reshape | solution.py:455
  2.7 1.0 %copy.19 = bf16[32,32,3,3]{0,3,2,1:T(4,128)(2,1)S(1)} copy(bf16[32,32,3,3]{1,0,3,2:T(8,128)(2,1)} %param.16) | data formatting | bytes 36864 | tf_op args[7]
  3.7 0.1 reshape.36
  3.8 0.7 %copy.22.w2_ref = bf16[32,288]{1,0:T(8,128)(2,1)} copy(bf16[32,288]{0,1:T(8,128)(2,1)S(1)} %reshape.36) | data formatting | bytes 36864 | tf_op jit(solution)/shard_map/reshape | solution.py:455
  4.5 48.4 %shard_map.128 = (f32[8,2048]{1,0:T(8,128)}, f32[8,2048]{1,0:T(8,128)}, f32[128,128]{1,0:T(8,128)}) custom-call(f32[8,2048]{1,0:T(8,128)} %est_ref.1, f32[128,128]{1,0:T(8,128)} %obs_ref.1, f32[8,2048]{1,0:T(8,128)} %cot_in_ref.1, s32[1,16]{1,0:T(1,128)} %zone_ref.1, s32[2,8]{1,0:T(2,128)} %pick_ref.1, f32[8,25]{1,0:T(8,128)} %psf_ref.1, ...), custom_call_target="tpu_custom_call" | custom-call | tf_op jit(solution)/shard_map/pallas_call | solution.py:409
  52.9 0.0 copy-start
  52.9 0.8 %slice_bitcast_fusion = f32[32,9]{0,1:T(8,128)S(1)} fusion(f32[128,128]{1,0:T(8,128)} %get-tuple-element.10), kind=kLoop, calls=%fused_computation | loop fusion | bytes 2304 | tf_op jit(solution)/shard_map/transpose | solution.py:459
  53.7 0.6 %reshape.43 = f32[1,32,3,3]{1,0,3,2:T(1,128)} reshape(f32[32,9]{0,1:T(8,128)S(1)} %slice_bitcast_fusion) | data formatting | bytes 2304 | tf_op jit(solution)/shard_map/reshape | solution.py:459
  54.3 0.8 %slice.12 = f32[32,9]{1,0:T(8,128)S(1)} slice(f32[128,128]{1,0:T(8,128)} %get-tuple-element.10), slice={[64:96], [32:41]} | slice | bytes 2304 | tf_op jit(solution)/shard_map/slice | solution.py:458
  55.1 0.0 copy-done
  55.1 0.1 copy.23
  55.2 0.6 %reshape.42 = f32[32,1,3,3]{0,1,3,2:T(1,128)} reshape(f32[32,9]{0,1:T(8,128)S(1)} %copy.23) | data formatting | bytes 2304 | tf_op jit(solution)/shard_map/reshape | solution.py:458
  55.8 0.1 reshape.38
  56.0 0.0 copy-start.2
  56.0 0.7 %slice.16 = f32[32,32,9]{1,0,2:T(8,128)} slice(f32[32,32,12]{1,0,2:T(8,128)S(1)} %bitcast.16), slice={[0:32], [0:32], [0:9]} | slice | bytes 73728 | tf_op jit(solution)/shard_map/slice | solution.py:457
  56.7 0.2 copy-done.2
  56.8 0.0 copy-start.1
  56.8 0.6 %copy.29 = f32[8,2048]{1,0:T(8,128)} copy(f32[8,2048]{1,0:T(8,128)S(1)} %copy-done.2) | data formatting | bytes 131072
  57.5 0.2 copy-done.1
  57.7 0.6 %copy.30 = f32[8,2048]{1,0:T(8,128)} copy(f32[8,2048]{1,0:T(8,128)S(1)} %copy-done.1) | data formatting | bytes 131072
  (3 shorter events, 0.0 us)
Async XLA Ops:
  1.3 0.7 %copy-start.3 = (bf16[1,32,3,3]{1,3,2,0:T(4,128)(2,1)S(1)}, bf16[1,32,3,3]{1,3,2,0:T(4,128)(2,1)}, u32[]{:S(2)}) copy-start(bf16[1,32,3,3]{1,3,2,0:T(4,128)(2,1)} %param.17) | copy-start | bytes 1732
  52.9 2.2 %copy-start = (f32[128,128]{1,0:T(8,128)S(1)}, f32[128,128]{1,0:T(8,128)}, u32[]{:S(2)}) copy-start(f32[128,128]{1,0:T(8,128)} %get-tuple-element.10) | copy-start | bytes 196612
  56.0 0.8 %copy-start.2 = (f32[8,2048]{1,0:T(8,128)S(1)}, f32[8,2048]{1,0:T(8,128)}, u32[]{:S(2)}) copy-start(f32[8,2048]{1,0:T(8,128)} %get-tuple-element.26) | copy-start | bytes 196612
  56.8 0.9 %copy-start.1 = (f32[8,2048]{1,0:T(8,128)S(1)}, f32[8,2048]{1,0:T(8,128)}, u32[]{:S(2)}) copy-start(f32[8,2048]{1,0:T(8,128)} %get-tuple-element.27) | copy-start | bytes 196612

commit v3 on v2

--- a/solution.py
+++ b/solution.py
@@ -39,6 +39,17 @@
     if delta == 1:
         return jnp.where(lane < width - 1, pltpu.roll(v, width - 1, 1), 0.0)
     return jnp.where(lane > 0, pltpu.roll(v, 1, 1), 0.0)
+
+
+def put_shifted(ref, rows, v, delta):
+    width = v.shape[1]
+    edge = width - 1 if delta == 1 else 0
+    ref[rows, :] = pltpu.roll(v, width - 1 if delta == 1 else 1, 1).astype(BF16)
+    ref[rows, edge : edge + 1] = jnp.zeros((v.shape[0], 1), BF16)
+
+
+def tn_dot(a, b):
+    return lax.dot_general(a, b, (((0,), (0,)), ((), ())), preferred_element_type=F32)
 
 
 def nt_dot(a, b):
@@ -74,7 +85,8 @@
         norm, hot[...], (((0,), (0,)), ((), ())), preferred_element_type=F32, precision=lax.Precision.HIGHEST)
 
 
-def build_weights(wf_ref, wl_ref, w2_ref, wsel, w1, wlt, wl3, wf3, wmb, wmtb):
+def build_weights(wfl_ref, w9_ref, w1, wlt, wl3, wf3, wmb, wmtb):
+    wf, wl = wfl_ref[0], wfl_ref[1]
     k, lane = iota((9, 48), 0), iota((9, 48), 1)
     ka = third(k, 3)
     kb = k - 3 * ka
@@ -92,9 +104,9 @@
         return ones_where(jnp.logical_and(same, hit))
 
     for i, r in enumerate(ROWS_14):
-        w1[i * 32 : i * 32 + 32, :] = jnp.dot(wf_ref[...], select(r, 1), preferred_element_type=F32).astype(BF16)
+        w1[i * 32 : i * 32 + 32, :] = tn_dot(wf, select(r, 1)).astype(BF16)
     for i, r in enumerate(ROWS_12):
-        wlt[i * 32 : i * 32 + 32, :] = jnp.dot(wl_ref[...], select(r, -1), preferred_element_type=F32).astype(BF16)
+        wlt[i * 32 : i * 32 + 32, :] = tn_dot(wl, select(r, -1)).astype(BF16)
     out, k = iota((24, 9), 0), iota((24, 9), 1)
     ob = third(out, 8)
     orow = out - 8 * ob
@@ -102,26 +114,20 @@
     same = k - 3 * ka == ob
     for i, q in enumerate(ROWS_10):
         fwd = ones_where(jnp.logical_and(same, ka == q - orow + 1))
-        wl3[:, i * 32 : i * 32 + 32] = nt_dot(fwd, wl_ref[...]).astype(BF16)
+        wl3[:, i * 32 : i * 32 + 32] = jnp.dot(fwd, wl, preferred_element_type=F32).astype(BF16)
         adj = ones_where(jnp.logical_and(same, ka == orow - q + 1))
-        wf3[:, i * 32 : i * 32 + 32] = nt_dot(adj, wf_ref[...]).astype(BF16)
-    k, m = iota((288, 288), 0), iota((288, 288), 1)
-    mb = third(m, 96)
-    rest = m - 96 * mb
-    ma = third(rest, 32)
-    order = ones_where(k == (rest - 32 * ma) * 9 + ma * 3 + mb)
-    wm = jnp.dot(w2_ref[...], order, preferred_element_type=F32).astype(BF16)
-    wsel[...] = wm
+        wf3[:, i * 32 : i * 32 + 32] = jnp.dot(adj, wf, preferred_element_type=F32).astype(BF16)
     eye = ones_where(iota((32, 32), 0) == iota((32, 32), 1))
     wmb[...] = jnp.zeros_like(wmb)
     wmtb[...] = jnp.zeros_like(wmtb)
     for b in range(3):
-        for r in range(12):
-            wmb[r * 32 : r * 32 + 32, b * 448 + r * 32 : b * 448 + r * 32 + 96] = wsel[:, b * 96 : b * 96 + 96]
-        turned = [nt_dot(eye, wsel[:, b * 96 + (2 - a) * 32 : b * 96 + (2 - a) * 32 + 32]) for a in range(3)]
+        line = jnp.concatenate([w9_ref[a * 3 + b] for a in range(3)], axis=1)
+        for r in range(6):
+            wmb[r * 32 : r * 32 + 32, b * 256 + r * 32 : b * 256 + r * 32 + 96] = line
+        turned = [nt_dot(eye, w9_ref[(2 - a) * 3 + b]) for a in range(3)]
         turned = jnp.concatenate(turned, axis=1).astype(BF16)
-        for r in range(10):
-            wmtb[r * 32 : r * 32 + 32, b * 384 + r * 32 : b * 384 + r * 32 + 96] = turned
+        for r in range(5):
+            wmtb[r * 32 : r * 32 + 32, b * 256 + r * 32 : b * 256 + r * 32 + 96] = turned
 
 
 def row_blur(values, tab):
@@ -176,11 +182,11 @@
 
 def kernel(
     n, scale,
-    est_ref, obs_ref, cot_in_ref, zone_ref, pick_ref, psf_ref, wf_ref, wl_ref, w2_ref,
-    den_ref, ge_ref, sums_ref,
+    est_ref, obs_ref, cot_in_ref, zone_ref, pick_ref, psf_ref, wfl_ref, w9_ref,
+    den_ref, ge_ref, gm_ref, gf_ref, gl_ref,
     tab, hot, send1, cols1, send2, back2, send3, cols3, send4, back4, share, share_in, whole, padded, adj,
     hx_send, hx_recv, ds_ref, cot_ref,
-    wsel, w1, wlt, wl3, wf3, wmb, wmtb, f3, c3, pre1, x3, pm, mid, bfr, d24, gm_acc, gf_acc, gl_acc,
+    w1, wlt, wl3, wf3, wmb, wmtb, f3, c3, pre1, x3, pm, mid, bfr, d24, gm_acc, gf_acc, gl_acc,
     send_sems, recv_sems, hs, hr,
 ):
     me = lax.axis_index("rows")
@@ -232,7 +238,7 @@
     for copy in near:
         copy.start()
     cols1[me] = send1[me]
-    build_weights(wf_ref, wl_ref, w2_ref, wsel, w1, wlt, wl3, wf3, wmb, wmtb)
+    build_weights(wfl_ref, w9_ref, w1, wlt, wl3, wf3, wmb, wmtb)
     arrive(copies1)
     column_pass(n, width, cols1, padded, adj, tab, obs_ref)
     sub = iota((BAND, BLK), 0)
@@ -286,13 +292,17 @@
         act, slope = silu_pair(pre1[grp(r), :].astype(F32))
         act = jnp.where(valid(r - 3), act, 0.0)
         pre1[grp(r), :] = slope.astype(pre1.dtype)
-        x3[grp(r), :] = shifted(act, -1).astype(BF16)
+        put_shifted(x3, grp(r), act.astype(BF16), -1)
         x3[grp(r + 14), :] = act.astype(BF16)
-        x3[grp(r + 28), :] = shifted(act, 1).astype(BF16)
+        put_shifted(x3, grp(r + 28), act.astype(BF16), 1)
 
     @pl.loop(0, chunks)
     def _(i):
-        pm[:, at(i)] = jnp.dot(wmb[...], x3[:, at(i)], preferred_element_type=F32).astype(pm.dtype)
+        for g in (0, 192):
+            total = jnp.dot(wmb[:, 0:256], x3[g : g + 256, at(i)], preferred_element_type=F32)
+            total = total + jnp.dot(wmb[:, 256:512], x3[448 + g : 704 + g, at(i)], preferred_element_type=F32)
+            total = total + jnp.dot(wmb[:, 512:768], x3[896 + g : 1152 + g, at(i)], preferred_element_type=F32)
+            pm[g : g + 192, at(i)] = total.astype(pm.dtype)
 
     @pl.loop(0, 12)
     def _(r):
@@ -317,25 +327,25 @@
     @pl.loop(0, 12)
     def _(r):
         back = pm[grp(r), :].astype(F32)
-        x3[grp(r), :] = shifted(back, 1).astype(BF16)
+        put_shifted(x3, grp(r), back.astype(BF16), 1)
         mid[grp(r), :] = back.astype(BF16)
-        x3[grp(r + 28), :] = shifted(back, -1).astype(BF16)
+        put_shifted(x3, grp(r + 28), back.astype(BF16), -1)
 
     gf_acc[...] = jnp.zeros_like(gf_acc)
-    row = iota((320, step), 0)
-    gone = jnp.logical_or(jnp.logical_and(row < 32, first), jnp.logical_and(row >= 288, last))
+    row = iota((160, step), 0)
 
     @pl.loop(0, chunks)
     def _(i):
-        back = (
-            jnp.dot(wmtb[:, 0:384], x3[0:384, at(i)], preferred_element_type=F32)
-            + jnp.dot(wmtb[:, 384:768], mid[:, at(i)], preferred_element_type=F32)
-            + jnp.dot(wmtb[:, 768:1152], x3[896:1280, at(i)], preferred_element_type=F32)
-        ) * pre1[64:384, at(i)].astype(F32)
-        back = jnp.where(gone, 0.0, back).astype(BF16)
-        bfr[...] = back
+        for g in (0, 160):
+            total = jnp.dot(wmtb[:, 0:224], x3[g : g + 224, at(i)], preferred_element_type=F32)
+            total = total + jnp.dot(wmtb[:, 256:480], mid[g : g + 224, at(i)], preferred_element_type=F32)
+            total = total + jnp.dot(wmtb[:, 512:736], x3[896 + g : 1120 + g, at(i)], preferred_element_type=F32)
+            total = total * pre1[64 + g : 224 + g, at(i)].astype(F32)
+            gone = jnp.logical_and(row < 32, first) if g == 0 else jnp.logical_and(row >= 128, last)
+            bfr[g : g + 160, :] = jnp.where(gone, 0.0, total).astype(BF16)
+        back = bfr[...]
         d24[:, at(i)] = jnp.dot(wf3[...], back, preferred_element_type=F32)
-        gf_acc[...] += nt_dot(bfr[32:288, :], f3[:, at(i)])
+        gf_acc[...] += nt_dot(f3[:, at(i)], bfr[32:288, :])
 
     ge_ref[...] = cot_ref[0:8, :] + d24[8:16, :] + shifted(d24[0:8, :], 1) + shifted(d24[16:24, :], -1)
     blurred = row_blur(ge_ref[...], tab)
@@ -361,13 +371,13 @@
                 total = total + gm_acc[b, r * 32 : r * 32 + 32, (r + a) * 32 : (r + a) * 32 + 32]
             slot = a * 3 + b
             share[slot // 4 * 32 : slot // 4 * 32 + 32, slot % 4 * 32 : slot % 4 * 32 + 32] = total * scale
-            total_first = jnp.zeros((32, 1), F32)
+            total_first = jnp.zeros((1, 32), F32)
             total_last = jnp.zeros((1, 32), F32)
             for r in range(8):
                 col = b * 16 + EXT_ROWS.index(r + a - 1)
-                total_first = total_first + gf_acc[r * 32 : r * 32 + 32, col : col + 1]
+                total_first = total_first + gf_acc[col : col + 1, r * 32 : r * 32 + 32]
                 total_last = total_last + gl_acc[b * 16 + r : b * 16 + r + 1, (r + a) * 32 : (r + a) * 32 + 32]
-            share[64:96, 32 + slot : 33 + slot] = total_first * scale
+            share[64 + slot : 65 + slot, 32:64] = total_first * scale
             share[64 + slot : 65 + slot, 64:96] = total_last * scale
 
     def eight(i):
@@ -390,8 +400,11 @@
     arrive(copies4)
     ge_ref[...] = ge_ref[...] - STEP_SIZE * row_blur_adjoint(back4, 8, n, width, tab)
     arrive(copies6)
-    for i in range(n):
-        sums_ref[i * 8 : i * 8 + 8, :] = whole[i]
+    for slot in range(9):
+        for q in range(4):
+            gm_ref[slot, q * 8 : q * 8 + 8, :] = whole[slot // 4 * 4 + q, :, slot % 4 * 32 : slot % 4 * 32 + 32]
+        gf_ref[slot] = whole[8 + slot // 8, slot % 8 : slot % 8 + 1, 32:64]
+        gl_ref[slot] = whole[8 + slot // 8, slot % 8 : slot % 8 + 1, 64:96]
     for copy in started + near:
         copy.wait_send()
 
@@ -406,15 +419,20 @@
     vmem, smem = pl.BlockSpec(memory_space=pltpu.VMEM), pl.BlockSpec(memory_space=pltpu.SMEM)
     block = pltpu.VMEM((n, 8, BLK), F32)
     tall = pltpu.VMEM((n, 16, BLK), F32)
-    denoised, grad_estimate, sums = pl.pallas_call(
+    ends = jnp.stack([
+        jnp.transpose(w_first, (2, 3, 1, 0)).reshape(9, CH), jnp.transpose(w_last, (2, 3, 0, 1)).reshape(9, CH)])
+    middle = jnp.transpose(w_mid, (2, 3, 0, 1)).reshape(9, CH, CH)
+    denoised, grad_estimate, grad_mid, grad_first, grad_last = pl.pallas_call(
         functools.partial(kernel, n, scale),
         out_shape=(
             jax.ShapeDtypeStruct((8, width), F32),
             jax.ShapeDtypeStruct((8, width), F32),
-            jax.ShapeDtypeStruct((8 * n, BLK), F32),
+            jax.ShapeDtypeStruct((9, CH, CH), F32),
+            jax.ShapeDtypeStruct((9, 1, CH), F32),
+            jax.ShapeDtypeStruct((9, 1, CH), F32),
         ),
-        in_specs=[vmem, vmem, vmem, smem, smem, vmem, vmem, vmem, vmem],
-        out_specs=[vmem] * 3,
+        in_specs=[vmem, vmem, vmem, smem, smem, vmem, vmem, vmem],
+        out_specs=[vmem] * 5,
         scratch_shapes=[
             pltpu.VMEM((32, table), F32),
             pltpu.VMEM((8, table), F32),
@@ -426,13 +444,12 @@
             pltpu.VMEM((2, 8, width), F32),
             pltpu.VMEM((16, width), F32),
             pltpu.VMEM((16, width), F32),
-            pltpu.VMEM((32, 288), BF16),
             pltpu.VMEM((448, 48), BF16),
             pltpu.VMEM((384, 48), BF16),
             pltpu.VMEM((24, 320), BF16),
             pltpu.VMEM((24, 320), BF16),
-            pltpu.VMEM((384, 1344), BF16),
-            pltpu.VMEM((320, 1152), BF16),
+            pltpu.VMEM((192, 768), BF16),
+            pltpu.VMEM((160, 768), BF16),
             pltpu.VMEM((48, width), BF16),
             pltpu.VMEM((48, width), BF16),
             pltpu.VMEM((448, width), keep),
@@ -442,7 +459,7 @@
             pltpu.VMEM((320, step), BF16),
             pltpu.VMEM((24, width), F32),
             pltpu.VMEM((3, 256, 320), F32),
-            pltpu.VMEM((256, 48), F32),
+            pltpu.VMEM((48, 256), F32),
             pltpu.VMEM((48, 320), F32),
             pltpu.SemaphoreType.DMA((6, n - 1)),
             pltpu.SemaphoreType.DMA((6, n - 1)),
@@ -452,11 +469,10 @@
         compiler_params=pltpu.CompilerParams(
             collective_id=0, has_side_effects=True, vmem_limit_bytes=56 << 20 if width <= 4096 else 64 << 20),
     )(estimate, observed, cotangent, zone_map, bank_pick, psf_bank,
-      w_first.reshape(32, 9), w_last.reshape(32, 9), w_mid.reshape(32, 288))
-    slots = sums[0:96].reshape(3, 32, 4, 32)
-    grad_mid = jnp.transpose(slots, (1, 3, 0, 2)).reshape(32, 32, 12)[:, :, 0:9].reshape(32, 32, 3, 3)
-    grad_first = sums[64:96, 32:41].reshape(32, 1, 3, 3)
-    grad_last = jnp.transpose(sums[64:73, 64:96]).reshape(1, 32, 3, 3)
+      ends, middle)
+    grad_mid = jnp.transpose(grad_mid.reshape(3, 3, CH, CH), (2, 3, 0, 1))
+    grad_first = jnp.transpose(grad_first.reshape(3, 3, 1, CH), (3, 2, 0, 1))
+    grad_last = jnp.transpose(grad_last.reshape(3, 3, 1, CH), (2, 3, 0, 1))
     return denoised, grad_estimate, grad_first, grad_mid, grad_last
 
 

time: 58.8 us -> 53.6 us (0.912)
  local copies, waits for them, and re-layouts: 9.26 us -> 6.25 us
  Pallas kernels: 48.4 us -> 45.8 us
  other arithmetic: 0 us -> 0.61 us
    reshape x10 -> x0, local copies, waits for them, and re-layouts: 4.22 us -> none  [the longest x2 1.39 us: on_device(): w_first.reshape(32, 9)]
    unnamed x11 -> x15, local copies, waits for them, and re-layouts: 2.65 us -> 6.22 us
    pallas_call x1, Pallas kernels: 48.4 us -> 45.8 us  [on_device(): pl.pallas_call(functools.partial(kernel, n, scale), out_shape=(jax.ShapeD...]
    slice x4 -> x0, local copies, waits for them, and re-layouts: 1.54 us -> none  [the longest x2 0.87 us: on_device(): grad_first = sums[64:96, 32:41].reshape(32, 1, 3, 3)]
    transpose x1 -> x0, local copies, waits for them, and re-layouts: 0.83 us -> none  [on_device(): grad_last = jnp.transpose(sums[64:73, 64:96]).reshape(1, 32, 3, 3)]
    another operation x0 -> x1, other arithmetic: none -> 0.61 us  [on_device(): jnp.stack([jnp.transpose(w_first, (2, 3, 1, 0)).reshape(9, CH), jnp.trans...]
where the time goes in v3:
time: 53.6 us; the launch traced here: 53.3 us
  Pallas kernels  45.8 us (85%)
  local copies, waits for them, and re-layouts  6.25 us (12%)
  between operations  0.66 us (1%)
  other arithmetic  0.61 us (1%)
    pallas_call x1, Pallas kernels, on_device(): pl.pallas_call(functools.partial(kernel, n, scale), out_shape=(jax.ShapeD...  45.8 us
    unnamed x15, local copies, waits for them, and re-layouts  6.22 us

profile of v3, /device:TPU:0, one launch (start us, length us, event | category | flops | bytes accessed | tf_op | source)
XLA Modules:
  0.0 53.3 jit_solution(7655143217196732903)
XLA Ops:
  0.6 0.0 copy-start.3
  0.6 0.7 %copy-done.3 = bf16[32,1,3,3]{0,3,2,1:T(4,128)(2,1)S(1)} copy-done((bf16[32,1,3,3]{0,3,2,1:T(4,128)(2,1)S(1)}, bf16[32,1,3,3]{0,3,2,1:T(4,128)(2,1)}, u32[]{:S(2)}) %copy-start.3) | copy-done | bytes 600
  1.3 0.0 copy-start.4
  1.3 0.7 %copy-done.4 = bf16[1,32,3,3]{1,3,2,0:T(4,128)(2,1)S(1)} copy-done((bf16[1,32,3,3]{1,3,2,0:T(4,128)(2,1)S(1)}, bf16[1,32,3,3]{1,3,2,0:T(4,128)(2,1)}, u32[]{:S(2)}) %copy-start.4) | copy-done | bytes 600
  2.0 0.6 %pad_maximum_fusion.wfl_ref = bf16[2,9,32]{2,1,0:T(8,128)(2,1)} fusion(bf16[1,9,32]{2,1,0:T(8,128)(2,1)S(1)} %stack_reshape.7, bf16[1,9,32]{2,1,0:T(8,128)(2,1)S(1)} %stack_reshape.6), kind=kLoop, calls=%fused_computation | loop fusion | flops 576 | bytes 2304 | tf_op jit(solution)/shard_map/stack | solution.py:422
  2.6 45.8 %shard_map.128 = (f32[8,2048]{1,0:T(8,128)}, f32[8,2048]{1,0:T(8,128)}, f32[9,32,32]{2,1,0:T(8,128)}, f32[9,1,32]{2,1,0:T(1,128)}, f32[9,1,32]{2,1,0:T(1,128)}) custom-call(f32[8,2048]{1,0:T(8,128)} %est_ref.1, f32[128,128]{1,0:T(8,128)} %obs_ref.1, f32[8,2048]{1,0:T(8,128)} %cot_in_ref.1, s32[1,16]{1,0:T(1,128)} %zone_ref.1, s32[2,8]{1,0:T(2,128)} %pick_ref.1, ...), custom_call_target="tpu_custom_call" | custom-call | tf_op jit(solution)/shard_map/pallas_call | solution.py:425
  48.4 0.0 copy-start
  48.4 1.5 %copy.19 = f32[8,2048]{1,0:T(8,128)} copy(f32[8,2048]{1,0:T(8,128)} %get-tuple-element.20) | data formatting | bytes 131072
  49.9 0.0 copy-start.2
  49.9 1.5 %copy.20 = f32[8,2048]{1,0:T(8,128)} copy(f32[8,2048]{1,0:T(8,128)} %get-tuple-element.21) | data formatting | bytes 131072
  51.4 0.0 copy-done.2
  51.4 0.6 %copy.21 = f32[32,1,3,3]{0,1,3,2:T(1,128)} copy(f32[32,1,3,3]{0,1,3,2:T(1,128)S(1)} %bitcast.21) | data formatting | bytes 2304
  52.0 0.0 copy-done
  52.0 0.0 copy-start.1
  52.0 0.7 %copy.22 = f32[32,32,3,3]{1,0,3,2:T(8,128)} copy(f32[32,32,3,3]{1,0,3,2:T(8,128)S(1)} %bitcast.18) | data formatting | bytes 73728
  52.7 0.0 copy-done.1
  52.7 0.6 %copy.23 = f32[1,32,3,3]{1,0,3,2:T(1,128)} copy(f32[1,32,3,3]{1,0,3,2:T(1,128)S(1)} %bitcast.20) | data formatting | bytes 2304
  (2 shorter events, 0.0 us)
Async XLA Ops:
  0.6 0.7 %copy-start.3 = (bf16[32,1,3,3]{0,3,2,1:T(4,128)(2,1)S(1)}, bf16[32,1,3,3]{0,3,2,1:T(4,128)(2,1)}, u32[]{:S(2)}) copy-start(bf16[32,1,3,3]{0,3,2,1:T(4,128)(2,1)} %param.15) | copy-start | bytes 1732
  1.3 0.7 %copy-start.4 = (bf16[1,32,3,3]{1,3,2,0:T(4,128)(2,1)S(1)}, bf16[1,32,3,3]{1,3,2,0:T(4,128)(2,1)}, u32[]{:S(2)}) copy-start(bf16[1,32,3,3]{1,3,2,0:T(4,128)(2,1)} %param.17) | copy-start | bytes 1732
  48.4 3.6 %copy-start = (f32[9,32,32]{2,1,0:T(8,128)S(1)}, f32[9,32,32]{2,1,0:T(8,128)}, u32[]{:S(2)}) copy-start(f32[9,32,32]{2,1,0:T(8,128)} %get-tuple-element.13) | copy-start | bytes 110596
  49.9 1.5 %copy-start.2 = (f32[9,1,32]{2,1,0:T(1,128)S(1)}, f32[9,1,32]{2,1,0:T(1,128)}, u32[]{:S(2)}) copy-start(f32[9,1,32]{2,1,0:T(1,128)} %get-tuple-element.12) | copy-start | bytes 3460
  52.0 0.7 %copy-start.1 = (f32[9,1,32]{2,1,0:T(1,128)S(1)}, f32[9,1,32]{2,1,0:T(1,128)}, u32[]{:S(2)}) copy-start(f32[9,1,32]{2,1,0:T(1,128)} %get-tuple-element.14) | copy-start | bytes 3460

commit v4 on v3

--- a/solution.py
+++ b/solution.py
@@ -142,7 +142,7 @@
 
 def row_blur_adjoint(back, rows, n, width, tab):
     end = width + BLK
-    wide = jnp.concatenate([back[j] for j in range(n)] + [jnp.zeros((rows, BLK), F32)], axis=1)
+    wide = jnp.concatenate([back[j].astype(F32) for j in range(n)] + [jnp.zeros((rows, BLK), F32)], axis=1)
     total = jnp.zeros((rows, end), F32)
     for t in range(TAPS):
         part = tab[t : t + 1, 0:end] * wide
@@ -155,7 +155,7 @@
     blocks = height // BLK
     padded[...] = jnp.zeros_like(padded)
     for i in range(n):
-        padded[16 + i * 8 : 24 + i * 8, :] = cols[i]
+        padded[16 + i * 8 : 24 + i * 8, :] = cols[i].astype(F32)
     results = []
     for blk in range(blocks):
         lanes = slice(width + (blk + 1) * BLK, width + (blk + 2) * BLK)
@@ -223,7 +223,7 @@
     build_table(n, tab, zone_ref, pick_ref, psf_ref, hot, width // BLK, BAND * n // BLK)
     blurred = row_blur(est_ref[...], tab)
     for j in range(n):
-        send1[j] = blurred[:, j * BLK : j * BLK + BLK]
+        send1[j] = blurred[:, j * BLK : j * BLK + BLK].astype(BF16)
     hx_send[0, 0:4, :] = est_ref[4:8, :]
     hx_send[0, 4:8, :] = cot_in_ref[4:8, :]
     hx_send[1, 0:4, :] = est_ref[0:4, :]
@@ -244,8 +244,8 @@
     sub = iota((BAND, BLK), 0)
     for i in range(n):
         base = 16 + i * 8
-        send2[i, 0:8, :] = adj[base : base + 8, :]
-        send2[i, 8:16, :] = jnp.where(sub < 4, adj[base - 4 : base + 4, :], adj[base + 4 : base + 12, :])
+        halo = jnp.where(sub < 4, adj[base - 4 : base + 4, :], adj[base + 4 : base + 12, :])
+        send2[i] = jnp.concatenate([adj[base : base + 8, :], halo], axis=0).astype(BF16)
     copies2 = exchange(1, lambda to: send2.at[to], back2)
     back2[me] = send2[me]
 
@@ -350,7 +350,7 @@
     ge_ref[...] = cot_ref[0:8, :] + d24[8:16, :] + shifted(d24[0:8, :], 1) + shifted(d24[16:24, :], -1)
     blurred = row_blur(ge_ref[...], tab)
     for j in range(n):
-        send3[j] = blurred[:, j * BLK : j * BLK + BLK]
+        send3[j] = blurred[:, j * BLK : j * BLK + BLK].astype(BF16)
     copies3 = exchange(2, lambda to: send3.at[to], cols3)
     cols3[me] = send3[me]
 
@@ -388,7 +388,7 @@
     arrive(copies3)
     column_pass(n, width, cols3, padded, adj, tab, None)
     for i in range(n):
-        send4[i] = adj[16 + i * 8 : 24 + i * 8, :]
+        send4[i] = adj[16 + i * 8 : 24 + i * 8, :].astype(BF16)
     copies4 = exchange(3, lambda to: send4.at[to], back4)
     back4[me] = send4[me]
     arrive(copies5)
@@ -418,7 +418,8 @@
     table = width + BLK + height
     vmem, smem = pl.BlockSpec(memory_space=pltpu.VMEM), pl.BlockSpec(memory_space=pltpu.SMEM)
     block = pltpu.VMEM((n, 8, BLK), F32)
-    tall = pltpu.VMEM((n, 16, BLK), F32)
+    flat = pltpu.VMEM((n, 8, BLK), BF16)
+    tall = pltpu.VMEM((n, 16, BLK), BF16)
     ends = jnp.stack([
         jnp.transpose(w_first, (2, 3, 1, 0)).reshape(9, CH), jnp.transpose(w_last, (2, 3, 0, 1)).reshape(9, CH)])
     middle = jnp.transpose(w_mid, (2, 3, 0, 1)).reshape(9, CH, CH)
@@ -436,7 +437,7 @@
         scratch_shapes=[
             pltpu.VMEM((32, table), F32),
             pltpu.VMEM((8, table), F32),
-            block, block, tall, tall, block, block, block, block,
+            flat, flat, tall, tall, flat, flat, flat, flat,
             pltpu.VMEM((8 * n, BLK), F32), block, block,
             pltpu.VMEM((max(height, BLK) + 64, BLK), F32),
             pltpu.VMEM((height + 32, BLK), F32),

time: 53.6 us -> 52.7 us (0.983)
  Pallas kernels: 45.8 us -> 44.8 us
    pallas_call x1, Pallas kernels: 45.8 us -> 44.8 us  [on_device(): pl.pallas_call(functools.partial(kernel, n, scale), out_shape=(jax.ShapeD...]
where the time goes in v4:
time: 52.7 us; the launch traced here: 52.4 us
  Pallas kernels  44.8 us (85%)
  local copies, waits for them, and re-layouts  6.25 us (12%)
  between operations  0.66 us (1%)
  other arithmetic  0.61 us (1%)
    pallas_call x1, Pallas kernels, on_device(): pl.pallas_call(functools.partial(kernel, n, scale), out_shape=(jax.ShapeD...  44.8 us
    unnamed x15, local copies, waits for them, and re-layouts  6.22 us

profile of v4, /device:TPU:0, one launch (start us, length us, event | category | flops | bytes accessed | tf_op | source)
XLA Modules:
  0.0 52.4 jit_solution(7620188530019502270)
XLA Ops:
  0.6 0.0 copy-start.3
  0.6 0.7 %copy-done.3 = bf16[32,1,3,3]{0,3,2,1:T(4,128)(2,1)S(1)} copy-done((bf16[32,1,3,3]{0,3,2,1:T(4,128)(2,1)S(1)}, bf16[32,1,3,3]{0,3,2,1:T(4,128)(2,1)}, u32[]{:S(2)}) %copy-start.3) | copy-done | bytes 600
  1.3 0.0 copy-start.4
  1.3 0.7 %copy-done.4 = bf16[1,32,3,3]{1,3,2,0:T(4,128)(2,1)S(1)} copy-done((bf16[1,32,3,3]{1,3,2,0:T(4,128)(2,1)S(1)}, bf16[1,32,3,3]{1,3,2,0:T(4,128)(2,1)}, u32[]{:S(2)}) %copy-start.4) | copy-done | bytes 600
  2.0 0.6 %pad_maximum_fusion.wfl_ref = bf16[2,9,32]{2,1,0:T(8,128)(2,1)} fusion(bf16[1,9,32]{2,1,0:T(8,128)(2,1)S(1)} %stack_reshape.7, bf16[1,9,32]{2,1,0:T(8,128)(2,1)S(1)} %stack_reshape.6), kind=kLoop, calls=%fused_computation | loop fusion | flops 576 | bytes 2304 | tf_op jit(solution)/shard_map/stack | solution.py:423
  2.6 44.8 %shard_map.128 = (f32[8,2048]{1,0:T(8,128)}, f32[8,2048]{1,0:T(8,128)}, f32[9,32,32]{2,1,0:T(8,128)}, f32[9,1,32]{2,1,0:T(1,128)}, f32[9,1,32]{2,1,0:T(1,128)}) custom-call(f32[8,2048]{1,0:T(8,128)} %est_ref.1, f32[128,128]{1,0:T(8,128)} %obs_ref.1, f32[8,2048]{1,0:T(8,128)} %cot_in_ref.1, s32[1,16]{1,0:T(1,128)} %zone_ref.1, s32[2,8]{1,0:T(2,128)} %pick_ref.1, ...), custom_call_target="tpu_custom_call" | custom-call | tf_op jit(solution)/shard_map/pallas_call | solution.py:426
  47.5 0.0 copy-start
  47.5 1.5 %copy.19 = f32[8,2048]{1,0:T(8,128)} copy(f32[8,2048]{1,0:T(8,128)} %get-tuple-element.20) | data formatting | bytes 131072
  49.0 0.0 copy-start.2
  49.0 1.5 %copy.20 = f32[8,2048]{1,0:T(8,128)} copy(f32[8,2048]{1,0:T(8,128)} %get-tuple-element.21) | data formatting | bytes 131072
  50.5 0.0 copy-done.2
  50.5 0.6 %copy.21 = f32[32,1,3,3]{0,1,3,2:T(1,128)} copy(f32[32,1,3,3]{0,1,3,2:T(1,128)S(1)} %bitcast.21) | data formatting | bytes 2304
  51.1 0.0 copy-done
  51.1 0.0 copy-start.1
  51.1 0.7 %copy.22 = f32[32,32,3,3]{1,0,3,2:T(8,128)} copy(f32[32,32,3,3]{1,0,3,2:T(8,128)S(1)} %bitcast.18) | data formatting | bytes 73728
  51.7 0.0 copy-done.1
  51.8 0.6 %copy.23 = f32[1,32,3,3]{1,0,3,2:T(1,128)} copy(f32[1,32,3,3]{1,0,3,2:T(1,128)S(1)} %bitcast.20) | data formatting | bytes 2304
  (2 shorter events, 0.0 us)
Async XLA Ops:
  0.6 0.7 %copy-start.3 = (bf16[32,1,3,3]{0,3,2,1:T(4,128)(2,1)S(1)}, bf16[32,1,3,3]{0,3,2,1:T(4,128)(2,1)}, u32[]{:S(2)}) copy-start(bf16[32,1,3,3]{0,3,2,1:T(4,128)(2,1)} %param.15) | copy-start | bytes 1732
  1.3 0.7 %copy-start.4 = (bf16[1,32,3,3]{1,3,2,0:T(4,128)(2,1)S(1)}, bf16[1,32,3,3]{1,3,2,0:T(4,128)(2,1)}, u32[]{:S(2)}) copy-start(bf16[1,32,3,3]{1,3,2,0:T(4,128)(2,1)} %param.17) | copy-start | bytes 1732
  47.5 3.6 %copy-start = (f32[9,32,32]{2,1,0:T(8,128)S(1)}, f32[9,32,32]{2,1,0:T(8,128)}, u32[]{:S(2)}) copy-start(f32[9,32,32]{2,1,0:T(8,128)} %get-tuple-element.13) | copy-start | bytes 110596
  49.0 1.5 %copy-start.2 = (f32[9,1,32]{2,1,0:T(1,128)S(1)}, f32[9,1,32]{2,1,0:T(1,128)}, u32[]{:S(2)}) copy-start(f32[9,1,32]{2,1,0:T(1,128)} %get-tuple-element.12) | copy-start | bytes 3460
  51.1 0.7 %copy-start.1 = (f32[9,1,32]{2,1,0:T(1,128)S(1)}, f32[9,1,32]{2,1,0:T(1,128)}, u32[]{:S(2)}) copy-start(f32[9,1,32]{2,1,0:T(1,128)} %get-tuple-element.14) | copy-start | bytes 3460
